TPU v7x, 256 devices: a whole 4x4x8 slice. The times are simulated.
256 devices in a mesh: side: 2 (over x_hi), row: 32 (over y, z), col: 4 (over x_lo, core).
Axes of the slice: x: 4 (x_hi: 2, x_lo: 2; x = x_hi * 2 + x_lo), y: 4, z: 8, core: 2. Of those that a mesh axis runs over, the one named last changes fastest.
Arguments:
- old_vectors: bfloat16 [2, 32768, 16384], P('side', 'row', 'col'), may hold values from -6 to 6
- reflectors: bfloat16 [2, 2, 32768, 512], P('side', None, 'row', 'col'), may hold values from -0.0625 to 0.0625
- triangles: float32 [2, 2, 512, 512], P('side'), may hold values from -0.25 to 0.25
- pole_sq: float32 [32768], replicated, may hold values from 1 to 65536, as said below
- coupling: float32 [32768], replicated, may hold values from -1 to 1
- deflated: int32 [32768], replicated, may hold values 0 or 1
- pole_order: int32 [32768], replicated, may hold values from 0 to 32767, each once
- anchors: int32 [1024], replicated, may hold values from 0 to 32766, as said below
- root_fraction: float32 [1024], replicated, may hold values from 0.2 to 0.8
Outputs:
- vectors: bfloat16 [2, 1024, 32768], P('side', 'col', 'row')
Inputs may be any that keep to these rules, and one draw needn't show every extreme that they name: `pole_sq`: strictly increasing; successive entries differ by 0.5 or more. `anchors`: distinct entries.
All inputs are finite; a program needn't handle non-finite values.
Results may differ from a plain program's by a relative error of at most 0.014.
Values may be sent and summed in bfloat16 or wider, within the bound.
A program may use at most 128 MiB of HBM per device.

v0:
```python
import jax
import jax.numpy as jnp
from jax import lax
from jax.sharding import PartitionSpec as P


def secular_columns(col_sq, col_coupling, col_live, weight, anchor_sq, pole_gap, root_fraction):
    denom = col_sq[:, None] - anchor_sq[None, :] - root_fraction[None, :] * pole_gap[None, :]
    return (col_live * col_coupling * weight)[:, None] / denom


def per_device(
    old_vectors,
    reflectors,
    triangles,
    pole_sq,
    coupling,
    deflated,
    pole_order,
    anchors,
    root_fraction,
):
    side_index = lax.axis_index("side")
    row_index = lax.axis_index("row")
    col_index = lax.axis_index("col")
    half_rows = lax.axis_size("row") // 2
    col_count = lax.axis_size("col")
    old_block = old_vectors[0]
    col_width = old_block.shape[1]
    order_size = pole_sq.shape[0]
    triplets = anchors.shape[0]
    local_triplets = triplets // col_count
    first_column = row_index // half_rows * (order_size // 2) + col_index * col_width
    columns = first_column + jnp.arange(col_width, dtype=jnp.int32)
    position = (
        jnp.zeros((order_size,), jnp.int32)
        .at[pole_order]
        .set(jnp.arange(order_size, dtype=jnp.int32))
    )
    sorted_pos = lax.dynamic_slice_in_dim(position, first_column, col_width)
    col_sq = pole_sq[sorted_pos]
    col_coupling = coupling[sorted_pos]
    col_live = (1 - deflated[sorted_pos]).astype(jnp.float32)
    weight = jnp.where(side_index == 0, jnp.ones_like(col_sq), jnp.sqrt(col_sq))
    anchor_sq = pole_sq[anchors]
    pole_gap = pole_sq[anchors + 1] - anchor_sq
    dead_triplet = deflated[anchors] == 1
    target = pole_order[anchors]
    secular = secular_columns(
        col_sq, col_coupling, col_live, weight, anchor_sq, pole_gap, root_fraction
    )
    onehot = (columns[:, None] == target[None, :]).astype(jnp.float32)
    mixing = jnp.where(dead_triplet[None, :], onehot, secular).astype(jnp.bfloat16)
    share_size = col_width // half_rows
    slice_part = lax.dynamic_slice_in_dim(
        secular, row_index % half_rows * share_size, share_size, 0
    )
    squares = lax.psum(jnp.sum(slice_part * slice_part, axis=0), ("row", "col"))
    col_scale = jnp.where(dead_triplet, jnp.ones_like(squares), 1.0 / jnp.sqrt(squares + 1e-06))
    merged = lax.psum_scatter(
        jnp.einsum("ck,rc->kr", mixing, old_block, preferred_element_type=jnp.float32).astype(
            jnp.bfloat16
        ),
        "col",
        scatter_dimension=0,
        tiled=True,
    ).astype(jnp.float32)
    my_scale = lax.dynamic_slice_in_dim(col_scale, col_index * local_triplets, local_triplets)
    vectors = merged * my_scale[:, None]
    panel_local = reflectors[0]
    panels = panel_local.shape[0]
    upper_tri = jnp.triu(triangles[0])
    highest = lax.Precision.HIGHEST
    for panel_index in reversed(range(panels)):
        panel_rows = panel_local[panel_index]
        current = vectors
        current_low = current.astype(jnp.bfloat16)
        projected = jnp.dot(
            current_low,
            lax.all_gather(panel_rows, "col", axis=1, tiled=True),
            preferred_element_type=jnp.float32,
        )
        projected = lax.psum(projected.astype(jnp.bfloat16), "row").astype(jnp.float32)
        coefficients = jnp.dot(projected, upper_tri[panel_index].T, precision=highest).astype(
            jnp.bfloat16
        )
        vectors = current - jnp.dot(
            coefficients,
            lax.all_gather(panel_rows, "col", axis=1, tiled=True).T,
            preferred_element_type=jnp.float32,
        )
    return vectors.astype(jnp.bfloat16)[None]


def solution(mesh):
    in_specs = (
        P("side", "row", "col"),
        P("side", None, "row", "col"),
        P("side", None, None, None),
        P(),
        P(),
        P(),
        P(),
        P(),
        P(),
    )
    out_specs = P("side", "col", "row")
    return jax.shard_map(
        per_device, mesh=mesh, in_specs=in_specs, out_specs=out_specs, check_vma=False
    )
```

profile of v0, /device:TPU:4, one launch (start us, length us, event | category | flops | bytes accessed | tf_op | source)
XLA Modules:
  0.0 883.0 jit_solution(16158088718118967877)
XLA Ops:
  6.5 0.0 copy-start
  6.5 0.0 all-gather.5.cloned.1.call-start
  6.5 1.9 fusion.23
  8.4 0.0 all-gather.5.cloned.1.call-update
  8.4 0.0 reduce-scatter.2.cloned.1.call-start
  8.5 0.9 compare_select_fusion
  9.5 120.1 %scatter_custom_fusion = s32[32768]{0:T(1024)S(1)} fusion(s32[32768]{0:T(1024)S(1)} %compare_select_fusion, s32[32768]{0:T(1024)S(1)} %iota.24, s32[]{:T(128)} %constant.23.clone.1), kind=kCustom, calls=%fused_computation.38 | custom fusion | bytes 131076 | tf_op jit(solution)/shard_map/scatter | solution.py:38
  129.6 0.0 copy-start.4
  129.6 0.0 copy-start.1
  129.6 19.5 %gather_fusion.2 = s32[4096]{0:T(1024)S(1)} fusion(s32[32768]{0:T(1024)} %param.14, s32[4096]{0:T(1024)S(1)} %fusion.20), kind=kCustom, calls=%fused_computation.2 | custom fusion | bytes 49152 | tf_op jit(solution)/shard_map/gather | solution.py:43
  149.2 0.0 copy-done
  149.2 0.0 copy-start.3
  149.2 0.0 copy-start.2
  149.2 23.0 %gather_fusion.4 = f32[4096]{0:T(1024)S(1)} fusion(f32[32768]{0:T(1024)S(1)} %copy-done, s32[4096]{0:T(1024)S(1)} %fusion.20), kind=kCustom, calls=%fused_computation.4 | custom fusion | bytes 49152 | tf_op jit(solution)/shard_map/gather | solution.py:41
  172.2 0.0 copy-done.4
  172.3 0.0 copy-start.5
  172.3 6.2 gather_fusion.5
  178.4 0.0 copy-done.1
  178.4 6.2 gather_fusion
  184.6 0.0 copy-done.3
  184.6 6.2 gather_fusion.1
  190.8 0.0 copy-done.2
  190.8 23.0 %gather_fusion.3 = f32[4096]{0:T(1024)S(1)} fusion(f32[32768]{0:T(1024)S(1)} %copy-done.2, s32[4096]{0:T(1024)S(1)} %fusion.20), kind=kCustom, calls=%fused_computation.3 | custom fusion | bytes 49152 | tf_op jit(solution)/shard_map/gather | solution.py:42
  213.8 6.2 gather_fusion.6
  220.0 6.5 subtract_divide_fusion
  226.5 1.3 multiply_reduce_fusion
  227.8 284.1 %psum.21 = f32[1024]{0:T(1024)S(1)} all-reduce(f32[1024]{0:T(1024)S(1)} %multiply_reduce_fusion), channel_id=1, replica_groups=mesh['side'=2,'row'=32,'col'=4] {'row','col'}, use_global_device_ids=true, to_apply=%region_3.4 | all-reduce | flops 1024 | bytes 8192 | tf_op jit(solution)/shard_map/psum | solution.py:58
  512.0 15.3 %fusion.5 = bf16[1024,1024]{1,0:T(8,128)(2,1)} fusion(bf16[1,1024,4096]{2,1,0:T(8,128)(2,1)} %param.9, s32[1024]{0:T(1024)S(1)} %gather_fusion.1, s32[4096]{0:T(1024)S(1)} %iota_add_fusion, pred[1024]{0:T(1024)(128)(4,1)S(1)} %get-tuple-element.6, f32[1024]{0:T(1024)S(1)} %subtract_multiply_fusion, f32[1024]{0:T(1024)S(1)} %gather_fusion.5, ...), kind=kOutput, calls=%fused_computation.16 | convolution fusion | flops 8620343296 | bytes 10548224 | tf_op jit(solution)/shard_map/ck,rc->kr/dot_general | solution.py:61
  527.3 0.0 reduce-scatter.2.cloned.1.call-update
  527.4 0.0 all-reduce.3.cloned.1.call-start
  527.4 0.1 dynamic_slice.11
  527.5 24.1 %reduce-scatter.2.cloned.1.call-done = bf16[256,1024]{1,0:T(8,128)(2,1)} async-done(((bf16[1024,1024]{1,0:T(8,128)(2,1)}), bf16[256,1024]{1,0:T(8,128)(2,1)}) %reduce-scatter.2.cloned.1.call-update) | async-done | bytes 524304 | tf_op jit(solution)/shard_map/reduce_scatter | solution.py:60
  551.6 2.6 convolution_convert_fusion.3
  554.2 0.0 all-reduce.3.cloned.1.call-update
  554.2 0.0 all-gather.7.cloned.1.call-start
  554.3 0.5 all-gather.7.cloned.1.call-update
  554.8 0.3 all-reduce.5.cloned.1.call-start
  555.1 0.2 iota_compare_fusion
  555.3 2.0 bitcast_select_fusion
  557.3 143.6 %all-reduce.3.cloned.1.call-done = bf16[256,512]{1,0:T(8,128)(2,1)} async-done(((bf16[256,512]{1,0:T(8,128)(2,1)}), bf16[256,512]{1,0:T(8,128)(2,1)}) %all-reduce.3.cloned.1.call-update) | async-done | bytes 262160 | tf_op jit(solution)/shard_map/psum | solution.py:83
  700.9 1.6 convolution_convert_fusion.2
  702.5 1.8 convolution_subtract_fusion.1
  704.4 18.7 %all-gather.7.cloned.1.call-done = bf16[1,1,1024,512]{3,2,1,0:T(8,128)(2,1)} async-done(((bf16[1,1,1024,128]{3,2,1,0:T(8,128)(2,1)}), bf16[1,1,1024,512]{3,2,1,0:T(8,128)(2,1)}) %all-gather.7.cloned.1.call-update) | async-done | bytes 1048592 | tf_op jit(solution)/shard_map/all_gather | solution.py:80
  723.1 2.4 convolution_convert_fusion.1
  725.5 0.0 all-reduce.5.cloned.1.call-update
  725.5 146.8 %all-reduce.5.cloned.1.call-done = bf16[256,512]{1,0:T(8,128)(2,1)} async-done(((bf16[256,512]{1,0:T(8,128)(2,1)}), bf16[256,512]{1,0:T(8,128)(2,1)}) %all-reduce.5.cloned.1.call-update) | async-done | bytes 262160 | tf_op jit(solution)/shard_map/psum | solution.py:83
  872.3 1.6 convolution_convert_fusion
  873.9 2.5 fusion.9
  (10 shorter events, 0.1 us)
Async XLA Ops:
  6.5 142.6 %copy-start = (f32[32768]{0:T(1024)S(1)}, f32[32768]{0:T(1024)}, u32[]{:S(2)}) copy-start(f32[32768]{0:T(1024)} %param.12) | copy-start | bytes 393220
  6.5 521.0 %all-gather.5.cloned.1.call-start = ((), (), s32[]{:S(2)}) async-start(), calls=%async_computation.4 | async-start | bytes 1310720 | tf_op jit(solution)/shard_map/all_gather | solution.py:80
  8.4 543.2 %reduce-scatter.2.cloned.1.call-start = ((), (), s32[]{:S(2)}) async-start(), calls=%async_computation.1 | async-start | bytes 2621440 | tf_op jit(solution)/shard_map/reduce_scatter | solution.py:60
  129.6 42.6 %copy-start.4 = (s32[1024]{0:T(1024)S(1)}, s32[1024]{0:T(1024)}, u32[]{:S(2)}) copy-start(s32[1024]{0:T(1024)} %param.16) | copy-start | bytes 12292
  129.6 48.8 %copy-start.1 = (s32[32768]{0:T(1024)S(1)}, s32[32768]{0:T(1024)}, u32[]{:S(2)}) copy-start(s32[32768]{0:T(1024)} %param.14) | copy-start | bytes 393220
  149.2 35.4 %copy-start.3 = (s32[32768]{0:T(1024)S(1)}, s32[32768]{0:T(1024)}, u32[]{:S(2)}) copy-start(s32[32768]{0:T(1024)} %param.15) | copy-start | bytes 393220
  149.2 41.6 %copy-start.2 = (f32[32768]{0:T(1024)S(1)}, f32[32768]{0:T(1024)}, u32[]{:S(2)}) copy-start(f32[32768]{0:T(1024)} %param.13) | copy-start | bytes 393220
  172.3 47.7 %copy-start.5 = (f32[1024]{0:T(1024)S(1)}, f32[1024]{0:T(1024)}, u32[]{:S(2)}) copy-start(f32[1024]{0:T(1024)} %param.17) | copy-start | bytes 12292
  527.4 173.5 %all-reduce.3.cloned.1.call-start = ((), (), s32[]{:S(2)}) async-start(), calls=%async_computation.2 | async-start | bytes 524288 | tf_op jit(solution)/shard_map/psum | solution.py:83
  554.2 168.9 %all-gather.7.cloned.1.call-start = ((), (), s32[]{:S(2)}) async-start(), calls=%async_computation.5 | async-start | bytes 1310720 | tf_op jit(solution)/shard_map/all_gather | solution.py:80
  554.8 317.5 %all-reduce.5.cloned.1.call-start = ((), (), s32[]{:S(2)}) async-start(), calls=%async_computation.3 | async-start | bytes 524288 | tf_op jit(solution)/shard_map/psum | solution.py:83
Sparse Core Ops, SparseCore 0:
  9.2 26.3 all-gather.4
  527.5 24.1 reduce-scatter.1
  555.5 145.3 all-reduce.2
  702.7 20.3 all-gather.6
  726.8 145.4 all-reduce.4
where the time goes:
time: 883 us
  waiting for transfers between devices  334 us (38%)
  blocking collectives  284 us (32%)
  local copies, waits for them, and re-layouts  212 us (24%)
  matrix products  27.8 us (3%)
  between operations  13.4 us (2%)
  other arithmetic  10.9 us (1%)
    psum x2, waiting for transfers between devices, per_device(): lax.psum(projected.astype(jnp.bfloat16), 'row').astype(jnp.float32)  290 us
    psum x1, blocking collectives, per_device(): squares = lax.psum(jnp.sum(slice_part * slice_part, axis=0), ('row', 'col'))  284 us
    scatter x1, local copies, waits for them, and re-layouts, per_device(): position = jnp.zeros((order_size,), jnp.int32).at[pole_order].set(jnp.ara...  120 us
    reduce_scatter x1, waiting for transfers between devices, per_device(): lax.psum_scatter(jnp.einsum('ck,rc->kr', mixing, old_block, preferred_ele...  24.1 us
    gather x1, local copies, waits for them, and re-layouts, per_device(): col_sq = pole_sq[sorted_pos]  23 us
    gather x1, local copies, waits for them, and re-layouts, per_device(): col_coupling = coupling[sorted_pos]  23 us
    gather x1, local copies, waits for them, and re-layouts, per_device(): col_live = (1 - deflated[sorted_pos]).astype(jnp.float32)  19.5 us
    all_gather x2, waiting for transfers between devices, per_device(): lax.all_gather(panel_rows, 'col', axis=1, tiled=True)  18.7 us
  transfers between devices with their start and end apart: 5, of which 4 were waited for; matrix products, arithmetic and copies ran while one was open for 27% of the time, Pallas kernels for 0%

commit v1 on v0

v1 whole, which is shorter than its diff:
```python
import functools

import jax
import jax.numpy as jnp
from jax import lax
from jax.experimental import pallas as pl
from jax.experimental.pallas import tpu as pltpu
from jax.sharding import PartitionSpec as P

LANES = 128
R_TILE = 256
PIECES = 3
F32 = jnp.float32
BF16 = jnp.bfloat16
MESH = pl.DeviceIdType.MESH
NT = (((1,), (1,)), ((), ()))
NN = (((1,), (0,)), ((), ()))


def dot(lhs, rhs, dims):
    return lax.dot_general(lhs, rhs, dims, preferred_element_type=F32)


def split3(value):
    high = value.astype(BF16).astype(F32)
    rest = value - high
    middle = rest.astype(BF16).astype(F32)
    return high, middle, rest - middle


def as_column(row):
    return jnp.broadcast_to(row.astype(F32), (LANES, LANES)).T


def kernel(
    cfg,
    old_hbm, refl_hbm, tri_hbm, pole_ref, coup_ref, defl_ref, order_ref, anchor_ref, frac_ref,
    out_ref,
    old_v, tri_v, v_parts, v_full, u_hi, u_lo, table, col_sq, col_num, asq_s, shift_s, code_s,
    mix, merged, on_send, on_recv, cr_send, cr_recv,
    rs_buf, y_recv, z_buf, z_recv, coef_buf,
    load_sem, v_send, v_recv, on_ssem, on_rsem, cr_ssem, cr_rsem,
    ys_sem, yr_sem, zs_sem, zr_sem, gz_ssem, gz_rsem, gy_ssem, gy_rsem,
):
    n_y, n_z, n_col, triplets, width, rows, n_panels, order_rows, panel = cfg
    own = triplets // n_col
    half_rows = n_y * n_z // 2
    n_hi = width // LANES
    n_rb = rows // R_TILE
    chunk = own // (n_y * n_z)
    blk = panel // n_col

    side = lax.axis_index("side")
    row = lax.axis_index("row")
    col = lax.axis_index("col")
    y, z = row // n_z, row % n_z
    x, core = col // 2, col % 2
    sib = {"col": x * 2 + 1 - core}
    across = {"col": (1 - x) * 2 + core}

    def y_peer(d):
        return lax.rem(y + d, n_y)

    def z_peer(d):
        return lax.rem(z + d, n_z)

    peers = [sib, across]
    peers += [{"row": y_peer(d) * n_z + z} for d in range(1, n_y)]
    peers += [{"row": y * n_z + z_peer(d)} for d in range(1, n_z)]

    barrier = pltpu.get_barrier_semaphore()
    for peer in peers:
        pl.semaphore_signal(barrier, inc=1, device_id=peer, device_id_type=MESH)

    load_old = pltpu.make_async_copy(old_hbm.at[0], old_v, load_sem.at[0])
    load_refl = pltpu.make_async_copy(refl_hbm.at[0], v_parts.at[col], load_sem.at[1])
    load_tri = pltpu.make_async_copy(tri_hbm.at[0], tri_v, load_sem.at[2])
    load_refl.start()
    load_old.start()
    load_tri.start()

    pl.semaphore_wait(barrier, len(peers))

    def remote(src, dst, ssem, rsem, peer):
        return pltpu.make_async_remote_copy(
            src_ref=src, dst_ref=dst, send_sem=ssem, recv_sem=rsem, device_id=peer, device_id_type=MESH
        )

    v_across = remote(refl_hbm.at[0], v_parts.at[col], v_send.at[0], v_recv.at[0], across)
    v_sib = remote(refl_hbm.at[0], v_parts.at[col], v_send.at[1], v_recv.at[1], sib)
    v_across.start()
    v_sib.start()

    first = row // half_rows * (width * n_col) + col * width
    sub_hi = lax.broadcasted_iota(jnp.int32, (n_hi, LANES), 0)
    sub_lo = lax.broadcasted_iota(jnp.int32, (LANES, LANES), 0)

    def scatter(g, acc):
        at = pl.ds(pl.multiple_of(g * 8, 8), 8)
        place = order_ref[at, :] - first
        hi, lo = place >> 7, place & (LANES - 1)
        live = (1 - defl_ref[at, :]).astype(F32) * coup_ref[at, :]
        values = split3(pole_ref[at, :]) + split3(live)
        left, right = [], []
        for r in range(8):
            mask = hi[r : r + 1, :] == sub_hi
            left.append(
                jnp.concatenate([jnp.where(mask, v[r : r + 1, :], 0.0) for v in values], axis=0).astype(BF16)
            )
            right.append(jnp.where(lo[r : r + 1, :] == sub_lo, 1.0, 0.0).astype(BF16))
        return acc + dot(jnp.concatenate(left, axis=1), jnp.concatenate(right, axis=1), NT)

    placed = lax.fori_loop(0, order_rows // 8, scatter, jnp.zeros((2 * PIECES * n_hi, LANES), F32))
    part = [placed[i * n_hi : (i + 1) * n_hi, :] for i in range(2 * PIECES)]
    sq = (part[0] + part[1]) + part[2]
    num = (part[3] + part[4]) + part[5]
    num = num * jnp.where(side == 0, jnp.ones_like(sq), jnp.sqrt(sq))
    for h in range(n_hi):
        lanes = slice(h * LANES, (h + 1) * LANES)
        col_sq[:, lanes] = jnp.broadcast_to(sq[h : h + 1, :], (8, LANES))
        col_num[:, lanes] = jnp.broadcast_to(num[h : h + 1, :], (8, LANES))

    pole = pole_ref[...]
    ahead = pltpu.roll(pole, LANES - 1, 1)
    wrapped = pltpu.roll(ahead, order_rows - 1, 0)
    lane_all = lax.broadcasted_iota(jnp.int32, (order_rows, LANES), 1)
    after = jnp.where(lane_all == LANES - 1, wrapped, ahead)
    order = order_ref[...]
    entries = split3(pole) + split3(after) + (
        (order >> 7).astype(F32), (order & (LANES - 1)).astype(F32), defl_ref[...].astype(F32),
    )
    for i, entry in enumerate(entries):
        table[:, i * LANES : (i + 1) * LANES] = entry.astype(BF16)
    lane_row = lax.broadcasted_iota(jnp.int32, (LANES, LANES), 1)
    lane_table = lax.broadcasted_iota(jnp.int32, (LANES, order_rows), 1)
    dead_mark = 65536.0

    for jb in range(triplets // LANES):
        anchor = as_column(anchor_ref[jb : jb + 1, :]).astype(jnp.int32)
        frac = as_column(frac_ref[jb : jb + 1, :])
        pick_hi = jnp.where((anchor >> 7)[:, :1] == lane_table, 1.0, 0.0).astype(BF16)
        found = dot(pick_hi, table[...], NN)
        f = [found[:, i * LANES : (i + 1) * LANES] for i in range(9)]
        pick_lo = (anchor & (LANES - 1)) == lane_row

        def chosen(value):
            return jnp.sum(jnp.where(pick_lo, value, 0.0), axis=1, keepdims=True)

        a_sq = chosen((f[0] + f[1]) + f[2])
        a_next = chosen((f[3] + f[4]) + f[5])
        target = chosen((f[6] * float(LANES) + f[7]) + f[8] * dead_mark)
        gap = a_next - a_sq
        code = jnp.where(target >= dead_mark, target - dead_mark - first.astype(F32), -dead_mark)
        at = slice(jb * LANES, (jb + 1) * LANES)
        asq_s[at, :] = jnp.broadcast_to(a_sq, (LANES, LANES))
        shift_s[at, :] = frac * gap
        code_s[at, :] = jnp.broadcast_to(code, (LANES, LANES))

    load_old.wait()
    lane_wide = lax.broadcasted_iota(jnp.int32, (8, width), 1).astype(F32)

    def make_mixing(first_triplet):
        def group(g, carry):
            parts = []
            for half in range(2):
                at = pl.ds(pl.multiple_of(first_triplet + g * 16 + half * 8, 8), 8)
                a_sq = jnp.tile(asq_s[at, :], (1, n_hi))
                shift = jnp.tile(shift_s[at, :], (1, n_hi))
                code = jnp.tile(code_s[at, :], (1, n_hi))
                den = (col_sq[...] - a_sq) - shift
                value = col_num[...] / den
                onehot = jnp.where(lane_wide == code, 1.0, 0.0)
                parts.append(jnp.where(code > -dead_mark, onehot, value))
            mix[pl.ds(pl.multiple_of(g * 16, 16), 16), :] = jnp.concatenate(parts, axis=0).astype(BF16)
            return carry

        lax.fori_loop(0, own // 16, group, 0)

    def product(rb):
        return dot(mix[...], old_v[pl.ds(pl.multiple_of(rb * R_TILE, R_TILE), R_TILE), :], NT)

    def on_copy(grp, rb):
        return remote(
            on_send.at[grp, rb], on_recv.at[grp, rb], on_ssem.at[grp, rb], on_rsem.at[grp, rb], sib
        )

    def cr_copy(rb):
        return remote(cr_send.at[rb], cr_recv.at[rb], cr_ssem.at[rb], cr_rsem.at[rb], across)

    v_fwd_at = (1 - x) * 2 + core
    v_fwd = remote(v_parts.at[v_fwd_at], v_parts.at[v_fwd_at], v_send.at[2], v_recv.at[2], sib)

    for grp in range(2):
        chip = 1 - x if grp == 0 else x
        make_mixing((chip * 2 + 1 - core) * own)

        def away(rb, carry):
            on_send[grp, rb] = product(rb).astype(BF16)
            on_copy(grp, rb).start()
            return carry

        lax.fori_loop(0, n_rb, away, 0)
        make_mixing((chip * 2 + core) * own)

        def home(rb, carry):
            value = product(rb)
            on_copy(grp, rb).wait()
            value = value + on_recv[grp, rb].astype(F32)
            if grp == 0:
                cr_send[rb] = value.astype(BF16)
                cr_copy(rb).start()
            else:
                merged[rb] = value
            return carry

        lax.fori_loop(0, n_rb, home, 0)
        if grp == 0:
            v_across.wait()
            v_fwd.start()

    my_rows = order_rows // (n_y * n_z)
    own_at = pl.ds(pl.multiple_of(col * own, LANES if own % LANES == 0 else 8), own)
    a_sq, shift = asq_s[own_at, :], shift_s[own_at, :]

    def square(r, acc):
        at = pl.ds(row * my_rows + r, 1)
        sq_row = pole_ref[at, :]
        weight = jnp.where(side == 0, jnp.ones_like(sq_row), jnp.sqrt(sq_row))
        num_row = (1 - defl_ref[at, :]).astype(F32) * coup_ref[at, :] * weight
        secular = num_row / ((sq_row - a_sq) - shift)
        return acc + secular * secular

    squares = lax.fori_loop(0, my_rows, square, jnp.zeros((own, LANES), F32))
    squares = jnp.sum(squares, axis=1, keepdims=True)
    lane_own = lax.broadcasted_iota(jnp.int32, (own, LANES), 1)

    def in_lanes(value, lane):
        pieces = split3(value)
        wide = jnp.where(lane == 0, pieces[0], 0.0)
        wide = jnp.where(lane == 1, pieces[1], wide)
        return jnp.where(lane == 2, pieces[2], wide)

    square_lanes = in_lanes(squares, lane_own)

    load_tri.wait()
    upper = lax.broadcasted_iota(jnp.int32, (panel, panel), 0) <= lax.broadcasted_iota(jnp.int32, (panel, panel), 1)
    for p in range(n_panels):
        u = jnp.where(upper, tri_v[p], 0.0)
        u_high = u.astype(BF16)
        u_hi[p] = u_high
        u_lo[p] = (u - u_high.astype(F32)).astype(BF16)

    load_refl.wait()
    v_sib.wait()
    v_fwd.wait()
    for p in range(n_panels):
        for c in range(n_col):
            v_full[p, :, c * blk : (c + 1) * blk] = v_parts[c, p]

    def arrive(rb, carry):
        cr_copy(rb).wait()
        merged[rb] = merged[rb] + cr_recv[rb].astype(F32)
        return carry

    lax.fori_loop(0, n_rb, arrive, 0)

    n_chunks = n_y * n_z
    lane_chunk = lax.broadcasted_iota(jnp.int32, (chunk, LANES), 1)

    for step in range(n_panels):
        p = n_panels - 1 - step

        def project(rb, acc):
            v_rows = v_full[p, pl.ds(pl.multiple_of(rb * R_TILE, R_TILE), R_TILE), :]
            return acc + dot(merged[rb].astype(BF16), v_rows, NN)

        proj = lax.fori_loop(0, n_rb, project, jnp.zeros((own, panel), F32))
        wide = jnp.concatenate([proj, square_lanes], axis=1)
        rs_buf[step] = wide.reshape(n_chunks, chunk, panel + LANES).astype(BF16)

        y_copies = [
            remote(
                rs_buf.at[step, pl.ds(y_peer(d) * n_z, n_z)], y_recv.at[step, d - 1],
                ys_sem.at[step, d - 1], yr_sem.at[step, d - 1], {"row": y_peer(d) * n_z + z},
            )
            for d in range(1, n_y)
        ]
        for copy in y_copies:
            copy.start()
        for copy in y_copies:
            copy.wait()
        total = rs_buf[step, pl.ds(y * n_z, n_z)].astype(F32)
        for d in range(1, n_y):
            total = total + y_recv[step, d - 1].astype(F32)
        z_buf[step] = total.astype(BF16)

        z_copies = [
            remote(
                z_buf.at[step, z_peer(d)], z_recv.at[step, d - 1],
                zs_sem.at[step, d - 1], zr_sem.at[step, d - 1], {"row": y * n_z + z_peer(d)},
            )
            for d in range(1, n_z)
        ]
        for copy in z_copies:
            copy.start()
        for copy in z_copies:
            copy.wait()
        total = z_buf[step, z].astype(F32)
        for d in range(1, n_z):
            total = total + z_recv[step, d - 1].astype(F32)

        proj_all = total[:, :panel]
        proj_hi = proj_all.astype(BF16).astype(F32)
        stacked = jnp.concatenate([proj_hi, proj_all - proj_hi], axis=0).astype(BF16)
        by_hi = dot(stacked, u_hi[p], NT)
        by_lo = dot(stacked, u_lo[p], NT)
        coef = by_hi[:chunk] + (by_hi[chunk:] + by_lo[:chunk])
        square_sum = jnp.sum(total[:, panel:], axis=1, keepdims=True)
        code = code_s[pl.ds(pl.multiple_of(col * own + row * chunk, 8), chunk), :1]
        scale = jnp.where(code > -dead_mark, 1.0, 1.0 / jnp.sqrt(square_sum + 1e-6))
        coef_buf[step, row] = jnp.concatenate([coef, in_lanes(scale, lane_chunk)], axis=1).astype(BF16)

        gz_copies = [
            remote(
                coef_buf.at[step, row], coef_buf.at[step, row],
                gz_ssem.at[step, d - 1], gz_rsem.at[step, d - 1], {"row": y * n_z + z_peer(d)},
            )
            for d in range(1, n_z)
        ]
        for copy in gz_copies:
            copy.start()
        for copy in gz_copies:
            copy.wait()
        gy_copies = [
            remote(
                coef_buf.at[step, pl.ds(y * n_z, n_z)], coef_buf.at[step, pl.ds(y * n_z, n_z)],
                gy_ssem.at[step, d - 1], gy_rsem.at[step, d - 1], {"row": y_peer(d) * n_z + z},
            )
            for d in range(1, n_y)
        ]
        for copy in gy_copies:
            copy.start()
        for copy in gy_copies:
            copy.wait()

        gathered = coef_buf[step].astype(F32).reshape(own, panel + LANES)
        coef_all = gathered[:, :panel].astype(BF16)
        last = step == n_panels - 1
        scale_all = jnp.sum(gathered[:, panel:], axis=1, keepdims=True)

        for rb in range(n_rb):
            at = slice(rb * R_TILE, (rb + 1) * R_TILE)
            value = merged[rb] - dot(coef_all, v_full[p, at, :], NT)
            if last:
                out_ref[0, :, at] = (value * scale_all).astype(BF16)
            else:
                merged[rb] = value


def per_device(cfg, old_vectors, reflectors, triangles, pole_sq, coupling, deflated, pole_order, anchors, root_fraction):
    n_y, n_z, n_col, triplets, width, rows, n_panels, order_rows, panel = cfg
    own = triplets // n_col
    n_rb = rows // R_TILE
    chunk = own // (n_y * n_z)
    lane_rows = lambda a: a.reshape(-1, LANES)
    dma, vmem = pltpu.SemaphoreType.DMA, pltpu.VMEM
    wide = panel + LANES
    scratch = [
        vmem((rows, width), BF16),
        vmem((n_panels, panel, panel), F32),
        vmem((n_col, n_panels, rows, panel // n_col), BF16),
        vmem((n_panels, rows, panel), BF16),
        vmem((n_panels, panel, panel), BF16),
        vmem((n_panels, panel, panel), BF16),
        vmem((order_rows, 9 * LANES), BF16),
        vmem((8, width), F32),
        vmem((8, width), F32),
        vmem((triplets, LANES), F32),
        vmem((triplets, LANES), F32),
        vmem((triplets, LANES), F32),
        vmem((own, width), BF16),
        vmem((n_rb, own, R_TILE), F32),
        vmem((2, n_rb, own, R_TILE), BF16),
        vmem((2, n_rb, own, R_TILE), BF16),
        vmem((n_rb, own, R_TILE), BF16),
        vmem((n_rb, own, R_TILE), BF16),
        vmem((n_panels, n_y * n_z, chunk, wide), BF16),
        vmem((n_panels, n_y - 1, n_z, chunk, wide), BF16),
        vmem((n_panels, n_z, chunk, wide), BF16),
        vmem((n_panels, n_z - 1, chunk, wide), BF16),
        vmem((n_panels, n_y * n_z, chunk, wide), BF16),
        dma((3,)), dma((3,)), dma((3,)),
        dma((2, n_rb)), dma((2, n_rb)), dma((n_rb,)), dma((n_rb,)),
        dma((n_panels, n_y - 1)), dma((n_panels, n_y - 1)),
        dma((n_panels, n_z - 1)), dma((n_panels, n_z - 1)),
        dma((n_panels, n_z - 1)), dma((n_panels, n_z - 1)),
        dma((n_panels, n_y - 1)), dma((n_panels, n_y - 1)),
    ]
    any_spec, vmem_spec = pl.BlockSpec(memory_space=pl.ANY), pl.BlockSpec(memory_space=pltpu.VMEM)
    return pl.pallas_call(
        functools.partial(kernel, cfg),
        out_shape=jax.ShapeDtypeStruct((1, own, rows), BF16),
        in_specs=[any_spec] * 3 + [vmem_spec] * 6,
        out_specs=vmem_spec,
        scratch_shapes=scratch,
        compiler_params=pltpu.CompilerParams(
            collective_id=0, has_side_effects=True, vmem_limit_bytes=56 << 20
        ),
    )(
        old_vectors, reflectors, triangles,
        lane_rows(pole_sq), lane_rows(coupling), lane_rows(deflated), lane_rows(pole_order),
        lane_rows(anchors), lane_rows(root_fraction),
    )


def solution(mesh):
    n_row, n_col = mesh.shape["row"], mesh.shape["col"]
    n_y = 4
    n_z = n_row // n_y

    def whole(old_vectors, reflectors, triangles, pole_sq, coupling, deflated, pole_order, anchors, root_fraction):
        size, panel = reflectors.shape[2:]
        cfg = (
            n_y, n_z, n_col, anchors.shape[0], old_vectors.shape[2] // n_col, size // n_row,
            reflectors.shape[1], size // LANES, panel,
        )
        in_specs = (P("side", "row", "col"), P("side", None, "row", "col"), P("side", None, None, None)) + (P(),) * 6
        return jax.shard_map(
            functools.partial(per_device, cfg), mesh=mesh, in_specs=in_specs,
            out_specs=P("side", "col", "row"), check_vma=False,
        )(old_vectors, reflectors, triangles, pole_sq, coupling, deflated, pole_order, anchors, root_fraction)

    return whole
```

time: 883 us -> 89.9 us (0.10)
  waiting for transfers between devices: 334 us -> 0 us
  blocking collectives: 284 us -> 0 us
  local copies, waits for them, and re-layouts: 212 us -> 1.87 us
  Pallas kernels: 0 us -> 87.9 us
  matrix products: 27.8 us -> 0 us
  between operations: 13.4 us -> 0.01 us
  other arithmetic: 10.9 us -> 0 us
    psum x2 -> x0, waiting for transfers between devices: 290 us -> none  [per_device(): lax.psum(projected.astype(jnp.bfloat16), 'row').astype(jnp.float32)]
    psum x1 -> x0, blocking collectives: 284 us -> none  [per_device(): squares = lax.psum(jnp.sum(slice_part * slice_part, axis=0), ('row', 'col'))]
    scatter x1 -> x0, local copies, waits for them, and re-layouts: 120 us -> none  [per_device(): position = jnp.zeros((order_size,), jnp.int32).at[pole_order].set(jnp.ara...]
    gather x7 -> x0, local copies, waits for them, and re-layouts: 90.2 us -> none  [the longest x1 23 us: per_device(): col_sq = pole_sq[sorted_pos]]
    pallas_call x0 -> x1, Pallas kernels: none -> 87.9 us  [per_device(): pl.pallas_call(functools.partial(kernel, cfg), out_shape=jax.ShapeDtypeSt...]
    dot_general x7 -> x0, matrix products: 27.8 us -> none  [the longest x1 15.3 us: per_device(): jnp.einsum('ck,rc->kr', mixing, old_block, preferred_element_type=jnp.flo...]
    reduce_scatter x1 -> x0, waiting for transfers between devices: 24.1 us -> none  [per_device(): lax.psum_scatter(jnp.einsum('ck,rc->kr', mixing, old_block, preferred_ele...]
    all_gather x2 -> x0, waiting for transfers between devices: 18.7 us -> none  [per_device(): lax.all_gather(panel_rows, 'col', axis=1, tiled=True)]
  transfers between devices with their start and end apart: 5 -> 0, of which waited for: 4 -> 0; matrix products, arithmetic and copies ran while one was open for 27% -> 0% of each run, Pallas kernels for 0% -> 0%
where the time goes in v1:
time: 89.9 us; the launch traced here: 89.7 us
  Pallas kernels  87.9 us (98%)
  local copies, waits for them, and re-layouts  1.87 us (2%)
    pallas_call x1, Pallas kernels, per_device(): pl.pallas_call(functools.partial(kernel, cfg), out_shape=jax.ShapeDtypeSt...  87.9 us
    unnamed x1, local copies, waits for them, and re-layouts  1.87 us

profile of v1, /device:TPU:4, one launch (start us, length us, event | category | flops | bytes accessed | tf_op | source)
XLA Modules:
  0.0 89.7 jit_solution(5235057820230272673)
XLA Ops:
  0.0 87.9 %shard_map.91 = bf16[1,256,1024]{2,1,0:T(8,128)(2,1)} custom-call(bf16[1,1024,4096]{2,1,0:T(8,128)(2,1)} %old_hbm.1, bf16[1,2,1024,128]{3,2,1,0:T(8,128)(2,1)} %refl_hbm.1, f32[1,2,512,512]{3,2,1,0:T(8,128)} %tri_hbm.1, f32[256,128]{1,0:T(8,128)} %bitcast.6, f32[256,128]{1,0:T(8,128)} %bitcast.7, s32[256,128]{1,0:T(8,128)} %bitcast.8, s32[256,128]{1,0:T(8,128)} %bitcast.9, ...), custom_call_target="tpu_custom_call" | custom-call | tf_op jit(solution)/shard_map/pallas_call | solution.py:400
  87.9 1.9 %copy.11 = bf16[1,256,1024]{2,1,0:T(8,128)(2,1)} copy(bf16[1,256,1024]{2,1,0:T(8,128)(2,1)} %shard_map.91) | data formatting | bytes 1048576

commit v2 on v1

v2 whole, which is shorter than its diff:
```python
import functools

import jax
import jax.numpy as jnp
from jax import lax
from jax.experimental import pallas as pl
from jax.experimental.pallas import tpu as pltpu
from jax.sharding import PartitionSpec as P

LANES = 128
R_TILE = 256
PIECES = 3
F32 = jnp.float32
BF16 = jnp.bfloat16
MESH = pl.DeviceIdType.MESH
NT = (((1,), (1,)), ((), ()))
NN = (((1,), (0,)), ((), ()))
TN = (((0,), (0,)), ((), ()))


def dot(lhs, rhs, dims):
    return lax.dot_general(lhs, rhs, dims, preferred_element_type=F32)


def split3(value):
    high = value.astype(BF16).astype(F32)
    rest = value - high
    middle = rest.astype(BF16).astype(F32)
    return high, middle, rest - middle


def as_column(row):
    return jnp.broadcast_to(row.astype(F32), (LANES, LANES)).T


def kernel(
    cfg,
    old_hbm, refl_hbm, tri_hbm, pole_ref, coup_ref, defl_ref, order_ref, anchor_ref, frac_ref,
    out_ref,
    old_v, tri_v, v_parts, v_full, u_hi, u_lo, table, col_sq, col_num, asq_s, shift_s, code_s, scale_s,
    mix, hold, merged, proj_acc, on_send, on_recv, cr_send, cr_recv, gram_all,
    sq_own, sq_y, sq_sum, sq_z,
    p_buf, p_y, p_z, p_zr, p_all, g_buf, g_y, g_z, g_zr, g_all,
    load_sem, v_send, v_recv, on_ssem, on_rsem, cr_ssem, cr_rsem, gram_ssem, gram_rsem,
    sy_ssem, sy_rsem, sz_ssem, sz_rsem,
    ys_sem, yr_sem, zs_sem, zr_sem, gz_ssem, gz_rsem, gy_ssem, gy_rsem,
):
    n_y, n_z, n_col, triplets, width, rows, n_panels, order_rows, panel = cfg
    own = triplets // n_col
    half_rows = n_y * n_z // 2
    n_chunks = n_y * n_z
    n_hi = width // LANES
    n_rb = rows // R_TILE
    chunk = own // n_chunks
    blk = panel // n_col
    half_panel = panel // 2
    g_chunk = half_panel // n_chunks
    scatter_rows = min(64, order_rows)

    side = lax.axis_index("side")
    row = lax.axis_index("row")
    col = lax.axis_index("col")
    y, z = row // n_z, row % n_z
    x, core = col // 2, col % 2
    sib = {"col": x * 2 + 1 - core}
    across = {"col": (1 - x) * 2 + core}

    def y_peer(d):
        return lax.rem(y + d, n_y)

    def z_peer(d):
        return lax.rem(z + d, n_z)

    def y_dev(d):
        return {"row": y_peer(d) * n_z + z}

    def z_dev(d):
        return {"row": y * n_z + z_peer(d)}

    peers = [sib, across] + [y_dev(d) for d in range(1, n_y)] + [z_dev(d) for d in range(1, n_z)]
    barrier = pltpu.get_barrier_semaphore()
    for peer in peers:
        pl.semaphore_signal(barrier, inc=1, device_id=peer, device_id_type=MESH)

    load_refl = pltpu.make_async_copy(refl_hbm.at[0], v_parts.at[col], load_sem.at[1])
    load_old = pltpu.make_async_copy(old_hbm.at[0], old_v, load_sem.at[0])
    load_tri = pltpu.make_async_copy(tri_hbm.at[0], tri_v, load_sem.at[2])
    load_refl.start()
    load_old.start()
    load_tri.start()

    def remote(src, dst, ssem, rsem, peer):
        return pltpu.make_async_remote_copy(
            src_ref=src, dst_ref=dst, send_sem=ssem, recv_sem=rsem, device_id=peer, device_id_type=MESH
        )

    first = row // half_rows * (width * n_col) + col * width
    sub_hi = lax.broadcasted_iota(jnp.int32, (n_hi, LANES), 0)
    sub_lo = lax.broadcasted_iota(jnp.int32, (LANES, LANES), 0)

    def scatter(g, acc):
        left, right = [], []
        for b in range(scatter_rows // 8):
            at = pl.ds(pl.multiple_of(g * scatter_rows + b * 8, 8), 8)
            place = order_ref[at, :] - first
            hi, lo = place >> 7, place & (LANES - 1)
            live = (1 - defl_ref[at, :]).astype(F32) * coup_ref[at, :]
            values = split3(pole_ref[at, :]) + split3(live)
            for r in range(8):
                mask = hi[r : r + 1, :] == sub_hi
                left.append(
                    jnp.concatenate([jnp.where(mask, v[r : r + 1, :], 0.0) for v in values], axis=0).astype(BF16)
                )
                right.append(jnp.where(lo[r : r + 1, :] == sub_lo, 1.0, 0.0).astype(BF16))
        return acc + dot(jnp.concatenate(left, axis=1), jnp.concatenate(right, axis=1), NT)

    placed = lax.fori_loop(
        0, order_rows // scatter_rows, scatter, jnp.zeros((2 * PIECES * n_hi, LANES), F32)
    )
    part = [placed[i * n_hi : (i + 1) * n_hi, :] for i in range(2 * PIECES)]
    sq = (part[0] + part[1]) + part[2]
    num = (part[3] + part[4]) + part[5]
    num = num * jnp.where(side == 0, jnp.ones_like(sq), jnp.sqrt(sq))
    for h in range(n_hi):
        lanes = slice(h * LANES, (h + 1) * LANES)
        col_sq[:, lanes] = jnp.broadcast_to(sq[h : h + 1, :], (8, LANES))
        col_num[:, lanes] = jnp.broadcast_to(num[h : h + 1, :], (8, LANES))

    pl.semaphore_wait(barrier, len(peers))

    v_across = remote(refl_hbm.at[0], v_parts.at[col], v_send.at[0], v_recv.at[0], across)
    v_sib = remote(refl_hbm.at[0], v_parts.at[col], v_send.at[1], v_recv.at[1], sib)
    v_across.start()
    v_sib.start()
    v_fwd_at = (1 - x) * 2 + core
    v_fwd = remote(v_parts.at[v_fwd_at], v_parts.at[v_fwd_at], v_send.at[2], v_recv.at[2], sib)

    pole = pole_ref[...]
    ahead = pltpu.roll(pole, LANES - 1, 1)
    wrapped = pltpu.roll(ahead, order_rows - 1, 0)
    lane_all = lax.broadcasted_iota(jnp.int32, (order_rows, LANES), 1)
    after = jnp.where(lane_all == LANES - 1, wrapped, ahead)
    order = order_ref[...]
    entries = split3(pole) + split3(after) + (
        (order >> 7).astype(F32), (order & (LANES - 1)).astype(F32), defl_ref[...].astype(F32),
    )
    for i, entry in enumerate(entries):
        table[:, i * LANES : (i + 1) * LANES] = entry.astype(BF16)
    lane_row = lax.broadcasted_iota(jnp.int32, (LANES, LANES), 1)
    lane_table = lax.broadcasted_iota(jnp.int32, (LANES, order_rows), 1)
    dead_mark = 65536.0

    for jb in range(triplets // LANES):
        anchor = as_column(anchor_ref[jb : jb + 1, :]).astype(jnp.int32)
        frac = as_column(frac_ref[jb : jb + 1, :])
        pick_hi = jnp.where((anchor >> 7)[:, :1] == lane_table, 1.0, 0.0).astype(BF16)
        found = dot(pick_hi, table[...], NN)
        f = [found[:, i * LANES : (i + 1) * LANES] for i in range(9)]
        pick_lo = (anchor & (LANES - 1)) == lane_row

        def chosen(value):
            return jnp.sum(jnp.where(pick_lo, value, 0.0), axis=1, keepdims=True)

        a_sq = chosen((f[0] + f[1]) + f[2])
        a_next = chosen((f[3] + f[4]) + f[5])
        target = chosen((f[6] * float(LANES) + f[7]) + f[8] * dead_mark)
        gap = a_next - a_sq
        code = jnp.where(target >= dead_mark, target - dead_mark - first.astype(F32), -dead_mark)
        at = slice(jb * LANES, (jb + 1) * LANES)
        asq_s[at, :] = jnp.broadcast_to(a_sq, (LANES, LANES))
        shift_s[at, :] = frac * gap
        code_s[at, :] = jnp.broadcast_to(code, (LANES, LANES))

    my_rows = order_rows // n_chunks
    own_at = pl.ds(pl.multiple_of(col * own, LANES), own)
    own_sq, own_shift = asq_s[own_at, :], shift_s[own_at, :]
    squares = jnp.zeros((own, LANES), F32)
    for r in range(my_rows):
        at = pl.ds(row * my_rows + r, 1)
        sq_row = pole_ref[at, :]
        weight = jnp.where(side == 0, jnp.ones_like(sq_row), jnp.sqrt(sq_row))
        num_row = (1 - defl_ref[at, :]).astype(F32) * coup_ref[at, :] * weight
        secular = num_row / ((sq_row - own_sq) - own_shift)
        squares = squares + secular * secular
    sq_own[...] = jnp.zeros((8, LANES), F32)
    for h in range(own // LANES):
        column = jnp.sum(squares[h * LANES : (h + 1) * LANES, :], axis=1, keepdims=True)
        sq_own[h : h + 1, :] = jnp.broadcast_to(column, (LANES, LANES)).T[:1, :]
    sy_copies = [
        remote(sq_own, sq_y.at[d - 1], sy_ssem.at[d - 1], sy_rsem.at[d - 1], y_dev(d)) for d in range(1, n_y)
    ]
    sz_copies = [
        remote(sq_sum, sq_z.at[d - 1], sz_ssem.at[d - 1], sz_rsem.at[d - 1], z_dev(d)) for d in range(1, n_z)
    ]
    for copy in sy_copies:
        copy.start()

    lane_wide = lax.broadcasted_iota(jnp.int32, (8, width), 1).astype(F32)

    def make_mixing(grp, g):
        chip = 1 - x if grp == 0 else x
        base = jnp.where(g < own // 16, (chip * 2 + 1 - core) * own, (chip * 2 + core) * own - own)
        parts = []
        for half in range(2):
            at = pl.ds(pl.multiple_of(base + g * 16 + half * 8, 8), 8)
            a_sq = jnp.tile(asq_s[at, :], (1, n_hi))
            shift = jnp.tile(shift_s[at, :], (1, n_hi))
            code = jnp.tile(code_s[at, :], (1, n_hi))
            den = (col_sq[...] - a_sq) - shift
            value = col_num[...] / den
            onehot = jnp.where(lane_wide == code, 1.0, 0.0)
            parts.append(jnp.where(code > -dead_mark, onehot, value))
        mix[grp, pl.ds(pl.multiple_of(g * 16, 16), 16), :] = jnp.concatenate(parts, axis=0).astype(BF16)

    def first_mixing(g, carry):
        make_mixing(0, g)
        return carry

    lax.fori_loop(0, own // 8, first_mixing, 0)
    load_old.wait()

    def product(grp, rb):
        return dot(mix[grp], old_v[pl.ds(pl.multiple_of(rb * R_TILE, R_TILE), R_TILE), :], NT)

    def on_copy(grp, rb):
        return remote(
            on_send.at[grp, rb], on_recv.at[grp, rb], on_ssem.at[grp, rb], on_rsem.at[grp, rb], sib
        )

    def cr_copy(rb):
        return remote(cr_send.at[rb], cr_recv.at[rb], cr_ssem.at[rb], cr_rsem.at[rb], across)

    def pass_across(rb):
        on_copy(0, rb).wait()
        cr_send[rb] = (hold[rb] + on_recv[0, rb].astype(F32)).astype(BF16)
        cr_copy(rb).start()

    per_rb = own // 8 // n_rb

    def other_chip(rb, carry):
        value = product(0, rb)
        for q in range(per_rb):
            make_mixing(1, rb * per_rb + q)
        on_send[0, rb] = value[:own].astype(BF16)
        on_copy(0, rb).start()
        hold[rb] = value[own:]

        @pl.when(rb > 0)
        def _():
            pass_across(rb - 1)

        return carry

    lax.fori_loop(0, n_rb, other_chip, 0)
    pass_across(n_rb - 1)

    for copy in sy_copies:
        copy.wait()
    total = sq_own[...]
    for d in range(1, n_y):
        total = total + sq_y[d - 1]
    sq_sum[...] = total
    for copy in sz_copies:
        copy.start()

    v_across.wait()
    v_fwd.start()

    def own_chip(rb, carry):
        value = product(1, rb)
        on_send[1, rb] = value[:own].astype(BF16)
        on_copy(1, rb).start()
        merged[rb] = value[own:]
        return carry

    lax.fori_loop(0, n_rb // 2, own_chip, 0)

    def reduction(i, buf, from_y, z_in, from_z, everything):
        y_out = [
            remote(buf.at[pl.ds(y_peer(d) * n_z, n_z)], from_y.at[d - 1], ys_sem.at[i, d - 1], yr_sem.at[i, d - 1], y_dev(d))
            for d in range(1, n_y)
        ]
        z_out = [
            remote(z_in.at[z_peer(d)], from_z.at[d - 1], zs_sem.at[i, d - 1], zr_sem.at[i, d - 1], z_dev(d))
            for d in range(1, n_z)
        ]
        mine = everything.at[row]
        z_back = [remote(mine, mine, gz_ssem.at[i, d - 1], gz_rsem.at[i, d - 1], z_dev(d)) for d in range(1, n_z)]
        line = everything.at[pl.ds(y * n_z, n_z)]
        y_back = [remote(line, line, gy_ssem.at[i, d - 1], gy_rsem.at[i, d - 1], y_dev(d)) for d in range(1, n_y)]

        def start(copies):
            for copy in copies:
                copy.start()

        def wait(copies):
            for copy in copies:
                copy.wait()

        def y_to_z():
            wait(y_out)
            summed = buf[pl.ds(y * n_z, n_z)].astype(F32)
            for d in range(1, n_y):
                summed = summed + from_y[d - 1].astype(F32)
            z_in[...] = summed.astype(BF16)
            start(z_out)

        def finish():
            wait(z_out)
            summed = z_in[z].astype(F32)
            for d in range(1, n_z):
                summed = summed + from_z[d - 1].astype(F32)
            return summed

        def send_back(value):
            everything[row] = value
            start(z_back)

        def z_to_y_back():
            wait(z_back)
            start(y_back)

        return (lambda: start(y_out)), y_to_z, finish, send_back, z_to_y_back, (lambda: wait(y_back))

    red_proj = [
        reduction(i, p_buf.at[i], p_y.at[i], p_z.at[i], p_zr.at[i], p_all.at[i]) for i in range(2)
    ]
    red_gram = reduction(2, g_buf, g_y, g_z, g_zr, g_all)

    load_refl.wait()
    v_sib.wait()
    v_fwd.wait()
    for p in range(n_panels):
        for c in range(n_col):
            v_full[p, :, c * blk : (c + 1) * blk] = v_parts[c, p]
    half_at = pl.ds(pl.multiple_of(core * half_panel, half_panel), half_panel)
    gram = dot(v_full[1, :, half_at], v_full[0], TN)
    g_buf[...] = gram.reshape(n_chunks, g_chunk, panel).astype(BF16)
    red_gram[0]()

    lax.fori_loop(n_rb // 2, n_rb, own_chip, 0)

    load_tri.wait()
    upper = lax.broadcasted_iota(jnp.int32, (panel, panel), 0) <= lax.broadcasted_iota(jnp.int32, (panel, panel), 1)
    for p in range(n_panels):
        u = jnp.where(upper, tri_v[p], 0.0)
        u_high = u.astype(BF16)
        u_hi[p] = u_high
        u_lo[p] = (u - u_high.astype(F32)).astype(BF16)
    red_gram[1]()

    for copy in sz_copies:
        copy.wait()
    total = sq_sum[...]
    for d in range(1, n_z):
        total = total + sq_z[d - 1]
    for h in range(own // LANES):
        scale = 1.0 / jnp.sqrt(as_column(total[h : h + 1, :]) + 1e-6)
        at = pl.ds(pl.multiple_of(col * own + h * LANES, LANES), LANES)
        scale_s[h * LANES : (h + 1) * LANES, :] = jnp.where(code_s[at, :] > -dead_mark, 1.0, scale)

    for rb in range(n_rb):
        at = slice(rb * R_TILE, (rb + 1) * R_TILE)
        on_copy(1, rb).wait()
        cr_copy(rb).wait()
        value = merged[rb] + on_recv[1, rb].astype(F32) + cr_recv[rb].astype(F32)
        merged[rb] = value
        value_low = value.astype(BF16)
        if rb < n_rb - 1:
            for p in range(2):
                term = dot(value_low, v_full[p, at, :], NN)
                proj_acc[p] = term if rb == 0 else proj_acc[p] + term
    for i in range(2):
        p = 1 - i
        term = proj_acc[p] + dot(value_low, v_full[p, at, :], NN)
        p_buf[i] = term.reshape(n_chunks, chunk, panel).astype(BF16)
        red_proj[i][0]()

    red_gram[3](red_gram[2]().astype(BF16))
    red_proj[0][1]()
    red_proj[1][1]()
    red_gram[4]()

    def apply_triangle(value, p):
        high = value.astype(BF16).astype(F32)
        stacked = jnp.concatenate([high, value - high], axis=0).astype(BF16)
        by_hi = dot(stacked, u_hi[p], NT)
        by_lo = dot(stacked, u_lo[p], NT)
        return (by_hi[:chunk] + (by_hi[chunk:] + by_lo[:chunk])).astype(BF16)

    coef_1 = apply_triangle(red_proj[0][2](), 1)
    red_proj[0][3](coef_1)
    red_gram[5]()
    gram_copy = remote(g_all, gram_all.at[core], gram_ssem, gram_rsem, sib)
    gram_copy.start()
    gram_all[core] = g_all[...]
    proj_0 = red_proj[1][2]()
    gram_copy.wait()
    gram_rows = gram_all[...].astype(F32).reshape(panel, panel).astype(BF16)
    coef_0 = apply_triangle(proj_0 - dot(coef_1, gram_rows, NN), 0)
    red_proj[1][3](coef_0)
    red_proj[0][4]()
    red_proj[1][4]()

    for i in range(2):
        p = 1 - i
        red_proj[i][5]()
        coef_all = p_all[i].astype(F32).reshape(own, panel).astype(BF16)
        for rb in range(n_rb):
            at = slice(rb * R_TILE, (rb + 1) * R_TILE)
            value = merged[rb] - dot(coef_all, v_full[p, at, :], NT)
            if i == 1:
                out_ref[0, :, at] = (value * jnp.tile(scale_s[...], (1, R_TILE // LANES))).astype(BF16)
            else:
                merged[rb] = value


def per_device(cfg, old_vectors, reflectors, triangles, pole_sq, coupling, deflated, pole_order, anchors, root_fraction):
    n_y, n_z, n_col, triplets, width, rows, n_panels, order_rows, panel = cfg
    own = triplets // n_col
    n_rb = rows // R_TILE
    chunk = own // (n_y * n_z)
    lane_rows = lambda a: a.reshape(-1, LANES)
    dma, vmem = pltpu.SemaphoreType.DMA, pltpu.VMEM
    n_row, half = n_y * n_z, panel // 2
    scratch = [
        vmem((rows, width), BF16),
        vmem((n_panels, panel, panel), F32),
        vmem((n_col, n_panels, rows, panel // n_col), BF16),
        vmem((n_panels, rows, panel), BF16),
        vmem((n_panels, panel, panel), BF16),
        vmem((n_panels, panel, panel), BF16),
        vmem((order_rows, 9 * LANES), BF16),
        vmem((8, width), F32),
        vmem((8, width), F32),
        vmem((triplets, LANES), F32),
        vmem((triplets, LANES), F32),
        vmem((triplets, LANES), F32),
        vmem((own, LANES), F32),
        vmem((2, 2 * own, width), BF16),
        vmem((n_rb, own, R_TILE), F32),
        vmem((n_rb, own, R_TILE), F32),
        vmem((2, own, panel), F32),
        vmem((2, n_rb, own, R_TILE), BF16),
        vmem((2, n_rb, own, R_TILE), BF16),
        vmem((n_rb, own, R_TILE), BF16),
        vmem((n_rb, own, R_TILE), BF16),
        vmem((2, n_row, half // n_row, panel), BF16),
        vmem((8, LANES), F32), vmem((n_y - 1, 8, LANES), F32),
        vmem((8, LANES), F32), vmem((n_z - 1, 8, LANES), F32),
        vmem((2, n_row, chunk, panel), BF16),
        vmem((2, n_y - 1, n_z, chunk, panel), BF16),
        vmem((2, n_z, chunk, panel), BF16),
        vmem((2, n_z - 1, chunk, panel), BF16),
        vmem((2, n_row, chunk, panel), BF16),
        vmem((n_row, half // n_row, panel), BF16),
        vmem((n_y - 1, n_z, half // n_row, panel), BF16),
        vmem((n_z, half // n_row, panel), BF16),
        vmem((n_z - 1, half // n_row, panel), BF16),
        vmem((n_row, half // n_row, panel), BF16),
        dma((3,)), dma((3,)), dma((3,)),
        dma((2, n_rb)), dma((2, n_rb)), dma((n_rb,)), dma((n_rb,)), dma, dma,
        dma((n_y - 1,)), dma((n_y - 1,)), dma((n_z - 1,)), dma((n_z - 1,)),
        dma((3, n_y - 1)), dma((3, n_y - 1)),
        dma((3, n_z - 1)), dma((3, n_z - 1)),
        dma((3, n_z - 1)), dma((3, n_z - 1)),
        dma((3, n_y - 1)), dma((3, n_y - 1)),
    ]
    any_spec, vmem_spec = pl.BlockSpec(memory_space=pl.ANY), pl.BlockSpec(memory_space=pltpu.VMEM)
    return pl.pallas_call(
        functools.partial(kernel, cfg),
        out_shape=jax.ShapeDtypeStruct((1, own, rows), BF16),
        in_specs=[any_spec] * 3 + [vmem_spec] * 6,
        out_specs=vmem_spec,
        scratch_shapes=scratch,
        compiler_params=pltpu.CompilerParams(
            collective_id=0, has_side_effects=True, vmem_limit_bytes=56 << 20
        ),
    )(
        old_vectors, reflectors, triangles,
        lane_rows(pole_sq), lane_rows(coupling), lane_rows(deflated), lane_rows(pole_order),
        lane_rows(anchors), lane_rows(root_fraction),
    )


def solution(mesh):
    n_row, n_col = mesh.shape["row"], mesh.shape["col"]
    n_y = 4
    n_z = n_row // n_y

    def whole(old_vectors, reflectors, triangles, pole_sq, coupling, deflated, pole_order, anchors, root_fraction):
        size, panel = reflectors.shape[2:]
        cfg = (
            n_y, n_z, n_col, anchors.shape[0], old_vectors.shape[2] // n_col, size // n_row,
            reflectors.shape[1], size // LANES, panel,
        )
        in_specs = (P("side", "row", "col"), P("side", None, "row", "col"), P("side", None, None, None)) + (P(),) * 6
        return jax.shard_map(
            functools.partial(per_device, cfg), mesh=mesh, in_specs=in_specs,
            out_specs=P("side", "col", "row"), check_vma=False,
        )(old_vectors, reflectors, triangles, pole_sq, coupling, deflated, pole_order, anchors, root_fraction)

    return whole
```

time: 89.9 us -> 66.2 us (0.74)
  Pallas kernels: 87.9 us -> 63.9 us
    pallas_call x1, Pallas kernels: 87.9 us -> 63.9 us  [per_device(): pl.pallas_call(functools.partial(kernel, cfg), out_shape=jax.ShapeDtypeSt...]
where the time goes in v2:
time: 66.2 us; the launch traced here: 65.7 us
  Pallas kernels  63.9 us (97%)
  local copies, waits for them, and re-layouts  1.87 us (3%)
    pallas_call x1, Pallas kernels, per_device(): pl.pallas_call(functools.partial(kernel, cfg), out_shape=jax.ShapeDtypeSt...  63.9 us
    unnamed x1, local copies, waits for them, and re-layouts  1.87 us

profile of v2, /device:TPU:4, one launch (start us, length us, event | category | flops | bytes accessed | tf_op | source)
XLA Modules:
  0.0 65.7 jit_solution(17939577482348810618)
XLA Ops:
  0.0 63.9 %shard_map.91 = bf16[1,256,1024]{2,1,0:T(8,128)(2,1)} custom-call(bf16[1,1024,4096]{2,1,0:T(8,128)(2,1)} %old_hbm.1, bf16[1,2,1024,128]{3,2,1,0:T(8,128)(2,1)} %refl_hbm.1, f32[1,2,512,512]{3,2,1,0:T(8,128)} %tri_hbm.1, f32[256,128]{1,0:T(8,128)} %bitcast.6, f32[256,128]{1,0:T(8,128)} %bitcast.7, s32[256,128]{1,0:T(8,128)} %bitcast.8, s32[256,128]{1,0:T(8,128)} %bitcast.9, ...), custom_call_target="tpu_custom_call" | custom-call | tf_op jit(solution)/shard_map/pallas_call | solution.py:470
  63.9 1.9 %copy.11 = bf16[1,256,1024]{2,1,0:T(8,128)(2,1)} copy(bf16[1,256,1024]{2,1,0:T(8,128)(2,1)} %shard_map.91) | data formatting | bytes 1048576

commit v3 on v2

--- a/solution.py
+++ b/solution.py
@@ -43,7 +43,7 @@
     p_buf, p_y, p_z, p_zr, p_all, g_buf, g_y, g_z, g_zr, g_all,
     load_sem, v_send, v_recv, on_ssem, on_rsem, cr_ssem, cr_rsem, gram_ssem, gram_rsem,
     sy_ssem, sy_rsem, sz_ssem, sz_rsem,
-    ys_sem, yr_sem, zs_sem, zr_sem, gz_ssem, gz_rsem, gy_ssem, gy_rsem,
+    ys_sem, yr_sem, zs_sem, zr_sem, gz_ssem, gz_rsem, gy_ssem, gy_rsem, meet_sem,
 ):
     n_y, n_z, n_col, triplets, width, rows, n_panels, order_rows, panel = cfg
     own = triplets // n_col
@@ -55,7 +55,7 @@
     blk = panel // n_col
     half_panel = panel // 2
     g_chunk = half_panel // n_chunks
-    scatter_rows = min(64, order_rows)
+    scatter_rows = min(128, order_rows)
 
     side = lax.axis_index("side")
     row = lax.axis_index("row")
@@ -77,7 +77,12 @@
     def z_dev(d):
         return {"row": y * n_z + z_peer(d)}
 
-    peers = [sib, across] + [y_dev(d) for d in range(1, n_y)] + [z_dev(d) for d in range(1, n_z)]
+    y_near = sorted({1, n_y - 1})
+    z_near = sorted({1, n_z - 1})
+    z_mid = sorted({d % n_z for d in (1, -1, 2, -2)} - {0})
+    near = [y_dev(d) for d in y_near] + [z_dev(d) for d in z_near]
+    middle = [z_dev(d) for d in z_mid]
+    peers = [sib, across] + near
     barrier = pltpu.get_barrier_semaphore()
     for peer in peers:
         pl.semaphore_signal(barrier, inc=1, device_id=peer, device_id_type=MESH)
@@ -93,6 +98,17 @@
         return pltpu.make_async_remote_copy(
             src_ref=src, dst_ref=dst, send_sem=ssem, recv_sem=rsem, device_id=peer, device_id_type=MESH
         )
+
+    pl.semaphore_wait(barrier, len(peers))
+    for peer in near:
+        pl.semaphore_signal(meet_sem.at[0], inc=1, device_id=peer, device_id_type=MESH)
+
+    v_across = remote(refl_hbm.at[0], v_parts.at[col], v_send.at[0], v_recv.at[0], across)
+    v_sib = remote(refl_hbm.at[0], v_parts.at[col], v_send.at[1], v_recv.at[1], sib)
+    v_across.start()
+    v_sib.start()
+    v_fwd_at = (1 - x) * 2 + core
+    v_fwd = remote(v_parts.at[v_fwd_at], v_parts.at[v_fwd_at], v_send.at[2], v_recv.at[2], sib)
 
     first = row // half_rows * (width * n_col) + col * width
     sub_hi = lax.broadcasted_iota(jnp.int32, (n_hi, LANES), 0)
@@ -126,14 +142,9 @@
         col_sq[:, lanes] = jnp.broadcast_to(sq[h : h + 1, :], (8, LANES))
         col_num[:, lanes] = jnp.broadcast_to(num[h : h + 1, :], (8, LANES))
 
-    pl.semaphore_wait(barrier, len(peers))
-
-    v_across = remote(refl_hbm.at[0], v_parts.at[col], v_send.at[0], v_recv.at[0], across)
-    v_sib = remote(refl_hbm.at[0], v_parts.at[col], v_send.at[1], v_recv.at[1], sib)
-    v_across.start()
-    v_sib.start()
-    v_fwd_at = (1 - x) * 2 + core
-    v_fwd = remote(v_parts.at[v_fwd_at], v_parts.at[v_fwd_at], v_send.at[2], v_recv.at[2], sib)
+    pl.semaphore_wait(meet_sem.at[0], len(near))
+    for peer in middle:
+        pl.semaphore_signal(meet_sem.at[1], inc=1, device_id=peer, device_id_type=MESH)
 
     pole = pole_ref[...]
     ahead = pltpu.roll(pole, LANES - 1, 1)
@@ -170,6 +181,173 @@
         asq_s[at, :] = jnp.broadcast_to(a_sq, (LANES, LANES))
         shift_s[at, :] = frac * gap
         code_s[at, :] = jnp.broadcast_to(code, (LANES, LANES))
+
+    pl.semaphore_wait(meet_sem.at[1], len(middle))
+
+    lane_wide = lax.broadcasted_iota(jnp.int32, (8, width), 1).astype(F32)
+
+    def make_mixing(grp, g):
+        chip = 1 - x if grp == 0 else x
+        base = jnp.where(g < own // 16, (chip * 2 + 1 - core) * own, (chip * 2 + core) * own - own)
+        parts = []
+        for half in range(2):
+            at = pl.ds(pl.multiple_of(base + g * 16 + half * 8, 8), 8)
+            a_sq = jnp.tile(asq_s[at, :], (1, n_hi))
+            shift = jnp.tile(shift_s[at, :], (1, n_hi))
+            code = jnp.tile(code_s[at, :], (1, n_hi))
+            den = (col_sq[...] - a_sq) - shift
+            value = col_num[...] / den
+            onehot = jnp.where(lane_wide == code, 1.0, 0.0)
+            parts.append(jnp.where(code > -dead_mark, onehot, value))
+        mix[grp, pl.ds(pl.multiple_of(g * 16, 16), 16), :] = jnp.concatenate(parts, axis=0).astype(BF16)
+
+    def first_mixing(g, carry):
+        make_mixing(0, g)
+        return carry
+
+    lax.fori_loop(0, own // 8, first_mixing, 0)
+    load_old.wait()
+
+    def product(grp, rb):
+        return dot(mix[grp], old_v[pl.ds(pl.multiple_of(rb * R_TILE, R_TILE), R_TILE), :], NT)
+
+    def on_copy(grp, rb):
+        return remote(
+            on_send.at[grp, rb], on_recv.at[grp, rb], on_ssem.at[grp, rb], on_rsem.at[grp, rb], sib
+        )
+
+    def cr_copy(rb):
+        return remote(cr_send.at[rb], cr_recv.at[rb], cr_ssem.at[rb], cr_rsem.at[rb], across)
+
+    def pass_across(rb):
+        on_copy(0, rb).wait()
+        cr_send[rb] = (hold[rb] + on_recv[0, rb].astype(F32)).astype(BF16)
+        cr_copy(rb).start()
+
+    per_rb = own // 8 // n_rb
+
+    def other_chip(rb, carry):
+        @pl.when(rb == n_rb - 1)
+        def _():
+            v_across.wait()
+            v_fwd.start()
+
+        value = product(0, rb)
+        for q in range(per_rb):
+            make_mixing(1, rb * per_rb + q)
+        on_send[0, rb] = value[:own].astype(BF16)
+        on_copy(0, rb).start()
+        hold[rb] = value[own:]
+
+        @pl.when(rb > 0)
+        def _():
+            pass_across(rb - 1)
+
+        return carry
+
+    lax.fori_loop(0, n_rb, other_chip, 0)
+    pass_across(n_rb - 1)
+
+    def own_chip(rb, carry):
+        value = product(1, rb)
+        on_send[1, rb] = value[:own].astype(BF16)
+        on_copy(1, rb).start()
+        merged[rb] = value[own:]
+        return carry
+
+    lax.fori_loop(0, n_rb // 2, own_chip, 0)
+
+    def reduction(i, buf, from_y, z_in, from_z, everything):
+        y_out = [
+            remote(buf.at[pl.ds(y_peer(d) * n_z, n_z)], from_y.at[d - 1], ys_sem.at[i, d - 1], yr_sem.at[i, d - 1], y_dev(d))
+            for d in range(1, n_y)
+        ]
+        z_out = [
+            remote(z_in.at[z_peer(d)], from_z.at[d - 1], zs_sem.at[i, d - 1], zr_sem.at[i, d - 1], z_dev(d))
+            for d in range(1, n_z)
+        ]
+        mine = everything.at[row]
+        z_back = [remote(mine, mine, gz_ssem.at[i, d - 1], gz_rsem.at[i, d - 1], z_dev(d)) for d in range(1, n_z)]
+        line = everything.at[pl.ds(y * n_z, n_z)]
+        y_back = [remote(line, line, gy_ssem.at[i, d - 1], gy_rsem.at[i, d - 1], y_dev(d)) for d in range(1, n_y)]
+
+        def start(copies):
+            for copy in copies:
+                copy.start()
+
+        def wait(copies):
+            for copy in copies:
+                copy.wait()
+
+        def y_to_z():
+            wait(y_out)
+            summed = buf[pl.ds(y * n_z, n_z)].astype(F32)
+            for d in range(1, n_y):
+                summed = summed + from_y[d - 1].astype(F32)
+            z_in[...] = summed.astype(BF16)
+            start(z_out)
+
+        def finish():
+            wait(z_out)
+            summed = z_in[z].astype(F32)
+            for d in range(1, n_z):
+                summed = summed + from_z[d - 1].astype(F32)
+            return summed
+
+        def send_back(value):
+            everything[row] = value
+            start(z_back)
+
+        def z_to_y_back():
+            wait(z_back)
+            start(y_back)
+
+        return (lambda: start(y_out)), y_to_z, finish, send_back, z_to_y_back, (lambda: wait(y_back))
+
+    red_proj = [
+        reduction(i, p_buf.at[i], p_y.at[i], p_z.at[i], p_zr.at[i], p_all.at[i]) for i in range(2)
+    ]
+    red_gram = reduction(2, g_buf, g_y, g_z, g_zr, g_all)
+
+    load_refl.wait()
+    v_sib.wait()
+    v_fwd.wait()
+    for p in range(n_panels):
+        for c in range(n_col):
+            v_full[p, :, c * blk : (c + 1) * blk] = v_parts[c, p]
+    half_at = pl.ds(pl.multiple_of(core * half_panel, half_panel), half_panel)
+    gram = dot(v_full[1, :, half_at], v_full[0], TN)
+    g_buf[...] = gram.reshape(n_chunks, g_chunk, panel).astype(BF16)
+    red_gram[0]()
+
+    lax.fori_loop(n_rb // 2, n_rb, own_chip, 0)
+
+    for rb in range(n_rb):
+        at = slice(rb * R_TILE, (rb + 1) * R_TILE)
+        if rb == n_rb - 1:
+            red_gram[1]()
+        on_copy(1, rb).wait()
+        cr_copy(rb).wait()
+        value = merged[rb] + on_recv[1, rb].astype(F32) + cr_recv[rb].astype(F32)
+        merged[rb] = value
+        value_low = value.astype(BF16)
+        if rb < n_rb - 1:
+            for p in range(2):
+                term = dot(value_low, v_full[p, at, :], NN)
+                proj_acc[p] = term if rb == 0 else proj_acc[p] + term
+    for i in range(2):
+        p = 1 - i
+        term = proj_acc[p] + dot(value_low, v_full[p, at, :], NN)
+        p_buf[i] = term.reshape(n_chunks, chunk, panel).astype(BF16)
+        red_proj[i][0]()
+
+    load_tri.wait()
+    upper = lax.broadcasted_iota(jnp.int32, (panel, panel), 0) <= lax.broadcasted_iota(jnp.int32, (panel, panel), 1)
+    for p in range(n_panels):
+        u = jnp.where(upper, tri_v[p], 0.0)
+        u_high = u.astype(BF16)
+        u_hi[p] = u_high
+        u_lo[p] = (u - u_high.astype(F32)).astype(BF16)
 
     my_rows = order_rows // n_chunks
     own_at = pl.ds(pl.multiple_of(col * own, LANES), own)
@@ -195,65 +373,9 @@
     for copy in sy_copies:
         copy.start()
 
-    lane_wide = lax.broadcasted_iota(jnp.int32, (8, width), 1).astype(F32)
-
-    def make_mixing(grp, g):
-        chip = 1 - x if grp == 0 else x
-        base = jnp.where(g < own // 16, (chip * 2 + 1 - core) * own, (chip * 2 + core) * own - own)
-        parts = []
-        for half in range(2):
-            at = pl.ds(pl.multiple_of(base + g * 16 + half * 8, 8), 8)
-            a_sq = jnp.tile(asq_s[at, :], (1, n_hi))
-            shift = jnp.tile(shift_s[at, :], (1, n_hi))
-            code = jnp.tile(code_s[at, :], (1, n_hi))
-            den = (col_sq[...] - a_sq) - shift
-            value = col_num[...] / den
-            onehot = jnp.where(lane_wide == code, 1.0, 0.0)
-            parts.append(jnp.where(code > -dead_mark, onehot, value))
-        mix[grp, pl.ds(pl.multiple_of(g * 16, 16), 16), :] = jnp.concatenate(parts, axis=0).astype(BF16)
-
-    def first_mixing(g, carry):
-        make_mixing(0, g)
-        return carry
-
-    lax.fori_loop(0, own // 8, first_mixing, 0)
-    load_old.wait()
-
-    def product(grp, rb):
-        return dot(mix[grp], old_v[pl.ds(pl.multiple_of(rb * R_TILE, R_TILE), R_TILE), :], NT)
-
-    def on_copy(grp, rb):
-        return remote(
-            on_send.at[grp, rb], on_recv.at[grp, rb], on_ssem.at[grp, rb], on_rsem.at[grp, rb], sib
-        )
-
-    def cr_copy(rb):
-        return remote(cr_send.at[rb], cr_recv.at[rb], cr_ssem.at[rb], cr_rsem.at[rb], across)
-
-    def pass_across(rb):
-        on_copy(0, rb).wait()
-        cr_send[rb] = (hold[rb] + on_recv[0, rb].astype(F32)).astype(BF16)
-        cr_copy(rb).start()
-
-    per_rb = own // 8 // n_rb
-
-    def other_chip(rb, carry):
-        value = product(0, rb)
-        for q in range(per_rb):
-            make_mixing(1, rb * per_rb + q)
-        on_send[0, rb] = value[:own].astype(BF16)
-        on_copy(0, rb).start()
-        hold[rb] = value[own:]
-
-        @pl.when(rb > 0)
-        def _():
-            pass_across(rb - 1)
-
-        return carry
-
-    lax.fori_loop(0, n_rb, other_chip, 0)
-    pass_across(n_rb - 1)
-
+    red_gram[3](red_gram[2]().astype(BF16))
+    red_proj[0][1]()
+    red_proj[1][1]()
     for copy in sy_copies:
         copy.wait()
     total = sq_own[...]
@@ -262,92 +384,27 @@
     sq_sum[...] = total
     for copy in sz_copies:
         copy.start()
-
-    v_across.wait()
-    v_fwd.start()
-
-    def own_chip(rb, carry):
-        value = product(1, rb)
-        on_send[1, rb] = value[:own].astype(BF16)
-        on_copy(1, rb).start()
-        merged[rb] = value[own:]
-        return carry
-
-    lax.fori_loop(0, n_rb // 2, own_chip, 0)
-
-    def reduction(i, buf, from_y, z_in, from_z, everything):
-        y_out = [
-            remote(buf.at[pl.ds(y_peer(d) * n_z, n_z)], from_y.at[d - 1], ys_sem.at[i, d - 1], yr_sem.at[i, d - 1], y_dev(d))
-            for d in range(1, n_y)
-        ]
-        z_out = [
-            remote(z_in.at[z_peer(d)], from_z.at[d - 1], zs_sem.at[i, d - 1], zr_sem.at[i, d - 1], z_dev(d))
-            for d in range(1, n_z)
-        ]
-        mine = everything.at[row]
-        z_back = [remote(mine, mine, gz_ssem.at[i, d - 1], gz_rsem.at[i, d - 1], z_dev(d)) for d in range(1, n_z)]
-        line = everything.at[pl.ds(y * n_z, n_z)]
-        y_back = [remote(line, line, gy_ssem.at[i, d - 1], gy_rsem.at[i, d - 1], y_dev(d)) for d in range(1, n_y)]
-
-        def start(copies):
-            for copy in copies:
-                copy.start()
-
-        def wait(copies):
-            for copy in copies:
-                copy.wait()
-
-        def y_to_z():
-            wait(y_out)
-            summed = buf[pl.ds(y * n_z, n_z)].astype(F32)
-            for d in range(1, n_y):
-                summed = summed + from_y[d - 1].astype(F32)
-            z_in[...] = summed.astype(BF16)
-            start(z_out)
-
-        def finish():
-            wait(z_out)
-            summed = z_in[z].astype(F32)
-            for d in range(1, n_z):
-                summed = summed + from_z[d - 1].astype(F32)
-            return summed
-
-        def send_back(value):
-            everything[row] = value
-            start(z_back)
-
-        def z_to_y_back():
-            wait(z_back)
-            start(y_back)
-
-        return (lambda: start(y_out)), y_to_z, finish, send_back, z_to_y_back, (lambda: wait(y_back))
-
-    red_proj = [
-        reduction(i, p_buf.at[i], p_y.at[i], p_z.at[i], p_zr.at[i], p_all.at[i]) for i in range(2)
-    ]
-    red_gram = reduction(2, g_buf, g_y, g_z, g_zr, g_all)
-
-    load_refl.wait()
-    v_sib.wait()
-    v_fwd.wait()
-    for p in range(n_panels):
-        for c in range(n_col):
-            v_full[p, :, c * blk : (c + 1) * blk] = v_parts[c, p]
-    half_at = pl.ds(pl.multiple_of(core * half_panel, half_panel), half_panel)
-    gram = dot(v_full[1, :, half_at], v_full[0], TN)
-    g_buf[...] = gram.reshape(n_chunks, g_chunk, panel).astype(BF16)
-    red_gram[0]()
-
-    lax.fori_loop(n_rb // 2, n_rb, own_chip, 0)
-
-    load_tri.wait()
-    upper = lax.broadcasted_iota(jnp.int32, (panel, panel), 0) <= lax.broadcasted_iota(jnp.int32, (panel, panel), 1)
-    for p in range(n_panels):
-        u = jnp.where(upper, tri_v[p], 0.0)
-        u_high = u.astype(BF16)
-        u_hi[p] = u_high
-        u_lo[p] = (u - u_high.astype(F32)).astype(BF16)
-    red_gram[1]()
+    red_gram[4]()
+
+    def apply_triangle(value, p):
+        high = value.astype(BF16).astype(F32)
+        stacked = jnp.concatenate([high, value - high], axis=0).astype(BF16)
+        by_hi = dot(stacked, u_hi[p], NT)
+        by_lo = dot(stacked, u_lo[p], NT)
+        return (by_hi[:chunk] + (by_hi[chunk:] + by_lo[:chunk])).astype(BF16)
+
+    red_gram[5]()
+    gram_copy = remote(g_all, gram_all.at[core], gram_ssem, gram_rsem, sib)
+    gram_copy.start()
+    gram_all[core] = g_all[...]
+    coef_1 = apply_triangle(red_proj[0][2](), 1)
+    red_proj[0][3](coef_1)
+    gram_copy.wait()
+    gram_rows = gram_all[...].astype(F32).reshape(panel, panel).astype(BF16)
+    carried = dot(coef_1, gram_rows, NN)
+    coef_0 = apply_triangle(red_proj[1][2]() - carried, 0)
+    red_proj[1][3](coef_0)
+    red_proj[0][4]()
 
     for copy in sz_copies:
         copy.wait()
@@ -359,47 +416,6 @@
         at = pl.ds(pl.multiple_of(col * own + h * LANES, LANES), LANES)
         scale_s[h * LANES : (h + 1) * LANES, :] = jnp.where(code_s[at, :] > -dead_mark, 1.0, scale)
 
-    for rb in range(n_rb):
-        at = slice(rb * R_TILE, (rb + 1) * R_TILE)
-        on_copy(1, rb).wait()
-        cr_copy(rb).wait()
-        value = merged[rb] + on_recv[1, rb].astype(F32) + cr_recv[rb].astype(F32)
-        merged[rb] = value
-        value_low = value.astype(BF16)
-        if rb < n_rb - 1:
-            for p in range(2):
-                term = dot(value_low, v_full[p, at, :], NN)
-                proj_acc[p] = term if rb == 0 else proj_acc[p] + term
-    for i in range(2):
-        p = 1 - i
-        term = proj_acc[p] + dot(value_low, v_full[p, at, :], NN)
-        p_buf[i] = term.reshape(n_chunks, chunk, panel).astype(BF16)
-        red_proj[i][0]()
-
-    red_gram[3](red_gram[2]().astype(BF16))
-    red_proj[0][1]()
-    red_proj[1][1]()
-    red_gram[4]()
-
-    def apply_triangle(value, p):
-        high = value.astype(BF16).astype(F32)
-        stacked = jnp.concatenate([high, value - high], axis=0).astype(BF16)
-        by_hi = dot(stacked, u_hi[p], NT)
-        by_lo = dot(stacked, u_lo[p], NT)
-        return (by_hi[:chunk] + (by_hi[chunk:] + by_lo[:chunk])).astype(BF16)
-
-    coef_1 = apply_triangle(red_proj[0][2](), 1)
-    red_proj[0][3](coef_1)
-    red_gram[5]()
-    gram_copy = remote(g_all, gram_all.at[core], gram_ssem, gram_rsem, sib)
-    gram_copy.start()
-    gram_all[core] = g_all[...]
-    proj_0 = red_proj[1][2]()
-    gram_copy.wait()
-    gram_rows = gram_all[...].astype(F32).reshape(panel, panel).astype(BF16)
-    coef_0 = apply_triangle(proj_0 - dot(coef_1, gram_rows, NN), 0)
-    red_proj[1][3](coef_0)
-    red_proj[0][4]()
     red_proj[1][4]()
 
     for i in range(2):
@@ -464,7 +480,7 @@
         dma((3, n_y - 1)), dma((3, n_y - 1)),
         dma((3, n_z - 1)), dma((3, n_z - 1)),
         dma((3, n_z - 1)), dma((3, n_z - 1)),
-        dma((3, n_y - 1)), dma((3, n_y - 1)),
+        dma((3, n_y - 1)), dma((3, n_y - 1)), pltpu.SemaphoreType.REGULAR((2,)),
     ]
     any_spec, vmem_spec = pl.BlockSpec(memory_space=pl.ANY), pl.BlockSpec(memory_space=pltpu.VMEM)
     return pl.pallas_call(

time: 66.2 us -> 68 us (1.027)
  Pallas kernels: 63.9 us -> 65.8 us
    pallas_call x1, Pallas kernels: 63.9 us -> 65.8 us  [per_device(): pl.pallas_call(functools.partial(kernel, cfg), out_shape=jax.ShapeDtypeSt...]
where the time goes in v3:
time: 68 us; the launch traced here: 67.7 us
  Pallas kernels  65.8 us (97%)
  local copies, waits for them, and re-layouts  1.87 us (3%)
    pallas_call x1, Pallas kernels, per_device(): pl.pallas_call(functools.partial(kernel, cfg), out_shape=jax.ShapeDtypeSt...  65.8 us
    unnamed x1, local copies, waits for them, and re-layouts  1.87 us

profile of v3, /device:TPU:4, one launch (start us, length us, event | category | flops | bytes accessed | tf_op | source)
XLA Modules:
  0.0 67.7 jit_solution(16390677095159788070)
XLA Ops:
  0.0 65.8 %shard_map.91 = bf16[1,256,1024]{2,1,0:T(8,128)(2,1)} custom-call(bf16[1,1024,4096]{2,1,0:T(8,128)(2,1)} %old_hbm.1, bf16[1,2,1024,128]{3,2,1,0:T(8,128)(2,1)} %refl_hbm.1, f32[1,2,512,512]{3,2,1,0:T(8,128)} %tri_hbm.1, f32[256,128]{1,0:T(8,128)} %bitcast.6, f32[256,128]{1,0:T(8,128)} %bitcast.7, s32[256,128]{1,0:T(8,128)} %bitcast.8, s32[256,128]{1,0:T(8,128)} %bitcast.9, ...), custom_call_target="tpu_custom_call" | custom-call | tf_op jit(solution)/shard_map/pallas_call | solution.py:486
  65.8 1.9 %copy.11 = bf16[1,256,1024]{2,1,0:T(8,128)(2,1)} copy(bf16[1,256,1024]{2,1,0:T(8,128)(2,1)} %shard_map.91) | data formatting | bytes 1048576

commit v4 on v3

--- a/solution.py
+++ b/solution.py
@@ -43,7 +43,7 @@
     p_buf, p_y, p_z, p_zr, p_all, g_buf, g_y, g_z, g_zr, g_all,
     load_sem, v_send, v_recv, on_ssem, on_rsem, cr_ssem, cr_rsem, gram_ssem, gram_rsem,
     sy_ssem, sy_rsem, sz_ssem, sz_rsem,
-    ys_sem, yr_sem, zs_sem, zr_sem, gz_ssem, gz_rsem, gy_ssem, gy_rsem, meet_sem,
+    ys_sem, yr_sem, zs_sem, zr_sem, b_ssem, b_rsem, meet_sem,
 ):
     n_y, n_z, n_col, triplets, width, rows, n_panels, order_rows, panel = cfg
     own = triplets // n_col
@@ -54,8 +54,8 @@
     chunk = own // n_chunks
     blk = panel // n_col
     half_panel = panel // 2
-    g_chunk = half_panel // n_chunks
-    scatter_rows = min(128, order_rows)
+    g_chunk = 2 * blk // n_chunks
+    scatter_rows = order_rows // 2
 
     side = lax.axis_index("side")
     row = lax.axis_index("row")
@@ -92,23 +92,11 @@
     load_tri = pltpu.make_async_copy(tri_hbm.at[0], tri_v, load_sem.at[2])
     load_refl.start()
     load_old.start()
-    load_tri.start()
 
     def remote(src, dst, ssem, rsem, peer):
         return pltpu.make_async_remote_copy(
             src_ref=src, dst_ref=dst, send_sem=ssem, recv_sem=rsem, device_id=peer, device_id_type=MESH
         )
-
-    pl.semaphore_wait(barrier, len(peers))
-    for peer in near:
-        pl.semaphore_signal(meet_sem.at[0], inc=1, device_id=peer, device_id_type=MESH)
-
-    v_across = remote(refl_hbm.at[0], v_parts.at[col], v_send.at[0], v_recv.at[0], across)
-    v_sib = remote(refl_hbm.at[0], v_parts.at[col], v_send.at[1], v_recv.at[1], sib)
-    v_across.start()
-    v_sib.start()
-    v_fwd_at = (1 - x) * 2 + core
-    v_fwd = remote(v_parts.at[v_fwd_at], v_parts.at[v_fwd_at], v_send.at[2], v_recv.at[2], sib)
 
     first = row // half_rows * (width * n_col) + col * width
     sub_hi = lax.broadcasted_iota(jnp.int32, (n_hi, LANES), 0)
@@ -130,9 +118,25 @@
                 right.append(jnp.where(lo[r : r + 1, :] == sub_lo, 1.0, 0.0).astype(BF16))
         return acc + dot(jnp.concatenate(left, axis=1), jnp.concatenate(right, axis=1), NT)
 
-    placed = lax.fori_loop(
-        0, order_rows // scatter_rows, scatter, jnp.zeros((2 * PIECES * n_hi, LANES), F32)
-    )
+    placed = scatter(0, jnp.zeros((2 * PIECES * n_hi, LANES), F32))
+
+    pl.semaphore_wait(barrier, len(peers))
+    for peer in near:
+        pl.semaphore_signal(meet_sem.at[0], inc=1, device_id=peer, device_id_type=MESH)
+
+    v_fwd_at = (1 - x) * 2 + core
+    v_across, v_fwd = [], []
+    for p in range(2):
+        v_across.append(remote(refl_hbm.at[0, p], v_parts.at[col, p], v_send.at[p], v_recv.at[p], across))
+        v_fwd.append(
+            remote(v_parts.at[v_fwd_at, p], v_parts.at[v_fwd_at, p], v_send.at[2 + p], v_recv.at[2 + p], sib)
+        )
+    v_sib = remote(refl_hbm.at[0], v_parts.at[col], v_send.at[4], v_recv.at[4], sib)
+    v_across[0].start()
+    v_sib.start()
+    load_tri.start()
+
+    placed = scatter(1, placed)
     part = [placed[i * n_hi : (i + 1) * n_hi, :] for i in range(2 * PIECES)]
     sq = (part[0] + part[1]) + part[2]
     num = (part[3] + part[4]) + part[5]
@@ -141,10 +145,6 @@
         lanes = slice(h * LANES, (h + 1) * LANES)
         col_sq[:, lanes] = jnp.broadcast_to(sq[h : h + 1, :], (8, LANES))
         col_num[:, lanes] = jnp.broadcast_to(num[h : h + 1, :], (8, LANES))
-
-    pl.semaphore_wait(meet_sem.at[0], len(near))
-    for peer in middle:
-        pl.semaphore_signal(meet_sem.at[1], inc=1, device_id=peer, device_id_type=MESH)
 
     pole = pole_ref[...]
     ahead = pltpu.roll(pole, LANES - 1, 1)
@@ -182,7 +182,10 @@
         shift_s[at, :] = frac * gap
         code_s[at, :] = jnp.broadcast_to(code, (LANES, LANES))
 
-    pl.semaphore_wait(meet_sem.at[1], len(middle))
+    v_across[1].start()
+    pl.semaphore_wait(meet_sem.at[0], len(near))
+    for peer in middle:
+        pl.semaphore_signal(meet_sem.at[1], inc=1, device_id=peer, device_id_type=MESH)
 
     lane_wide = lax.broadcasted_iota(jnp.int32, (8, width), 1).astype(F32)
 
@@ -224,38 +227,11 @@
         cr_send[rb] = (hold[rb] + on_recv[0, rb].astype(F32)).astype(BF16)
         cr_copy(rb).start()
 
-    per_rb = own // 8 // n_rb
-
-    def other_chip(rb, carry):
-        @pl.when(rb == n_rb - 1)
-        def _():
-            v_across.wait()
-            v_fwd.start()
-
-        value = product(0, rb)
-        for q in range(per_rb):
-            make_mixing(1, rb * per_rb + q)
-        on_send[0, rb] = value[:own].astype(BF16)
-        on_copy(0, rb).start()
-        hold[rb] = value[own:]
-
-        @pl.when(rb > 0)
-        def _():
-            pass_across(rb - 1)
-
-        return carry
-
-    lax.fori_loop(0, n_rb, other_chip, 0)
-    pass_across(n_rb - 1)
-
-    def own_chip(rb, carry):
-        value = product(1, rb)
-        on_send[1, rb] = value[:own].astype(BF16)
-        on_copy(1, rb).start()
-        merged[rb] = value[own:]
-        return carry
-
-    lax.fori_loop(0, n_rb // 2, own_chip, 0)
+    far = [(dy, dz) for dy in range(n_y) for dz in range(n_z) if dy or dz]
+    far.sort(key=lambda d: -(min(d[0], n_y - d[0]) + min(d[1], n_z - d[1])))
+
+    def far_dev(dy, dz):
+        return {"row": y_peer(dy) * n_z + z_peer(dz)}
 
     def reduction(i, buf, from_y, z_in, from_z, everything):
         y_out = [
@@ -267,9 +243,7 @@
             for d in range(1, n_z)
         ]
         mine = everything.at[row]
-        z_back = [remote(mine, mine, gz_ssem.at[i, d - 1], gz_rsem.at[i, d - 1], z_dev(d)) for d in range(1, n_z)]
-        line = everything.at[pl.ds(y * n_z, n_z)]
-        y_back = [remote(line, line, gy_ssem.at[i, d - 1], gy_rsem.at[i, d - 1], y_dev(d)) for d in range(1, n_y)]
+        back = [remote(mine, mine, b_ssem.at[i, k], b_rsem.at[i, k], far_dev(dy, dz)) for k, (dy, dz) in enumerate(far)]
 
         def start(copies):
             for copy in copies:
@@ -296,58 +270,56 @@
 
         def send_back(value):
             everything[row] = value
-            start(z_back)
-
-        def z_to_y_back():
-            wait(z_back)
-            start(y_back)
-
-        return (lambda: start(y_out)), y_to_z, finish, send_back, z_to_y_back, (lambda: wait(y_back))
+            start(back)
+
+        return (lambda: start(y_out)), y_to_z, finish, send_back, (lambda: wait(back))
 
     red_proj = [
         reduction(i, p_buf.at[i], p_y.at[i], p_z.at[i], p_zr.at[i], p_all.at[i]) for i in range(2)
     ]
     red_gram = reduction(2, g_buf, g_y, g_z, g_zr, g_all)
 
-    load_refl.wait()
-    v_sib.wait()
-    v_fwd.wait()
-    for p in range(n_panels):
+    per_rb = own // 8 // n_rb
+
+    def assemble(p):
         for c in range(n_col):
             v_full[p, :, c * blk : (c + 1) * blk] = v_parts[c, p]
-    half_at = pl.ds(pl.multiple_of(core * half_panel, half_panel), half_panel)
-    gram = dot(v_full[1, :, half_at], v_full[0], TN)
-    g_buf[...] = gram.reshape(n_chunks, g_chunk, panel).astype(BF16)
-    red_gram[0]()
-
-    lax.fori_loop(n_rb // 2, n_rb, own_chip, 0)
-
-    for rb in range(n_rb):
-        at = slice(rb * R_TILE, (rb + 1) * R_TILE)
-        if rb == n_rb - 1:
-            red_gram[1]()
-        on_copy(1, rb).wait()
-        cr_copy(rb).wait()
-        value = merged[rb] + on_recv[1, rb].astype(F32) + cr_recv[rb].astype(F32)
-        merged[rb] = value
-        value_low = value.astype(BF16)
-        if rb < n_rb - 1:
-            for p in range(2):
-                term = dot(value_low, v_full[p, at, :], NN)
-                proj_acc[p] = term if rb == 0 else proj_acc[p] + term
-    for i in range(2):
-        p = 1 - i
-        term = proj_acc[p] + dot(value_low, v_full[p, at, :], NN)
-        p_buf[i] = term.reshape(n_chunks, chunk, panel).astype(BF16)
-        red_proj[i][0]()
-
-    load_tri.wait()
-    upper = lax.broadcasted_iota(jnp.int32, (panel, panel), 0) <= lax.broadcasted_iota(jnp.int32, (panel, panel), 1)
-    for p in range(n_panels):
-        u = jnp.where(upper, tri_v[p], 0.0)
-        u_high = u.astype(BF16)
-        u_hi[p] = u_high
-        u_lo[p] = (u - u_high.astype(F32)).astype(BF16)
+
+    v_across[0].wait()
+    v_fwd[0].start()
+
+    def other_chip(rb, carry):
+        @pl.when(rb == n_rb - 1)
+        def _():
+            v_across[1].wait()
+            v_fwd[1].start()
+
+        @pl.when(rb == 1)
+        def _():
+            load_refl.wait()
+            v_sib.wait()
+            v_fwd[0].wait()
+            assemble(0)
+            gram = dot(v_parts[col, 1], v_full[0], TN)
+            gram = jnp.concatenate([gram[:, :half_panel], gram[:, half_panel:]], axis=0)
+            g_buf[...] = gram.reshape(n_chunks, g_chunk, half_panel).astype(BF16)
+            red_gram[0]()
+
+        value = product(0, rb)
+        for q in range(per_rb):
+            make_mixing(1, rb * per_rb + q)
+        on_send[0, rb] = value[:own].astype(BF16)
+        on_copy(0, rb).start()
+        hold[rb] = value[own:]
+
+        @pl.when(rb > 0)
+        def _():
+            pass_across(rb - 1)
+
+        return carry
+
+    lax.fori_loop(0, n_rb, other_chip, 0)
+    pass_across(n_rb - 1)
 
     my_rows = order_rows // n_chunks
     own_at = pl.ds(pl.multiple_of(col * own, LANES), own)
@@ -370,12 +342,48 @@
     sz_copies = [
         remote(sq_sum, sq_z.at[d - 1], sz_ssem.at[d - 1], sz_rsem.at[d - 1], z_dev(d)) for d in range(1, n_z)
     ]
+    pl.semaphore_wait(meet_sem.at[1], len(middle))
     for copy in sy_copies:
         copy.start()
-
+    red_gram[1]()
+
+    def own_chip(rb, carry):
+        value = product(1, rb)
+        on_send[1, rb] = value[:own].astype(BF16)
+        on_copy(1, rb).start()
+        merged[rb] = value[own:]
+        return carry
+
+    lax.fori_loop(0, n_rb, own_chip, 0)
+    v_fwd[1].wait()
+    assemble(1)
     red_gram[3](red_gram[2]().astype(BF16))
-    red_proj[0][1]()
-    red_proj[1][1]()
+
+    for rb in range(n_rb):
+        at = slice(rb * R_TILE, (rb + 1) * R_TILE)
+        on_copy(1, rb).wait()
+        cr_copy(rb).wait()
+        value = merged[rb] + on_recv[1, rb].astype(F32) + cr_recv[rb].astype(F32)
+        merged[rb] = value
+        value_low = value.astype(BF16)
+        if rb < n_rb - 1:
+            for p in range(2):
+                term = dot(value_low, v_full[p, at, :], NN)
+                proj_acc[p] = term if rb == 0 else proj_acc[p] + term
+    for i in range(2):
+        p = 1 - i
+        term = proj_acc[p] + dot(value_low, v_full[p, at, :], NN)
+        p_buf[i] = term.reshape(n_chunks, chunk, panel).astype(BF16)
+        red_proj[i][0]()
+
+    load_tri.wait()
+    upper = lax.broadcasted_iota(jnp.int32, (panel, panel), 0) <= lax.broadcasted_iota(jnp.int32, (panel, panel), 1)
+    for p in range(n_panels):
+        u = jnp.where(upper, tri_v[p], 0.0)
+        u_high = u.astype(BF16)
+        u_hi[p] = u_high
+        u_lo[p] = (u - u_high.astype(F32)).astype(BF16)
+
     for copy in sy_copies:
         copy.wait()
     total = sq_own[...]
@@ -384,7 +392,9 @@
     sq_sum[...] = total
     for copy in sz_copies:
         copy.start()
-    red_gram[4]()
+
+    red_proj[0][1]()
+    red_proj[1][1]()
 
     def apply_triangle(value, p):
         high = value.astype(BF16).astype(F32)
@@ -393,19 +403,27 @@
         by_lo = dot(stacked, u_lo[p], NT)
         return (by_hi[:chunk] + (by_hi[chunk:] + by_lo[:chunk])).astype(BF16)
 
-    red_gram[5]()
-    gram_copy = remote(g_all, gram_all.at[core], gram_ssem, gram_rsem, sib)
-    gram_copy.start()
-    gram_all[core] = g_all[...]
+    red_gram[4]()
+    diagonal = {"col": (1 - x) * 2 + 1 - core}
+    gram_copies = [
+        remote(g_all, gram_all.at[col], gram_ssem.at[i], gram_rsem.at[i], peer)
+        for i, peer in enumerate((across, diagonal, sib))
+    ]
+    for copy in gram_copies:
+        copy.start()
+    gram_all[col] = g_all[...]
     coef_1 = apply_triangle(red_proj[0][2](), 1)
     red_proj[0][3](coef_1)
-    gram_copy.wait()
-    gram_rows = gram_all[...].astype(F32).reshape(panel, panel).astype(BF16)
+    gram_rows = []
+    for copy in gram_copies:
+        copy.wait()
+    for c in range(n_col):
+        quarter = gram_all[c].astype(F32).reshape(2 * blk, half_panel)
+        gram_rows.append(jnp.concatenate([quarter[:blk], quarter[blk:]], axis=1))
+    gram_rows = jnp.concatenate(gram_rows, axis=0).astype(BF16)
     carried = dot(coef_1, gram_rows, NN)
     coef_0 = apply_triangle(red_proj[1][2]() - carried, 0)
     red_proj[1][3](coef_0)
-    red_proj[0][4]()
-
     for copy in sz_copies:
         copy.wait()
     total = sq_sum[...]
@@ -416,11 +434,9 @@
         at = pl.ds(pl.multiple_of(col * own + h * LANES, LANES), LANES)
         scale_s[h * LANES : (h + 1) * LANES, :] = jnp.where(code_s[at, :] > -dead_mark, 1.0, scale)
 
-    red_proj[1][4]()
-
     for i in range(2):
         p = 1 - i
-        red_proj[i][5]()
+        red_proj[i][4]()
         coef_all = p_all[i].astype(F32).reshape(own, panel).astype(BF16)
         for rb in range(n_rb):
             at = slice(rb * R_TILE, (rb + 1) * R_TILE)
@@ -439,6 +455,7 @@
     lane_rows = lambda a: a.reshape(-1, LANES)
     dma, vmem = pltpu.SemaphoreType.DMA, pltpu.VMEM
     n_row, half = n_y * n_z, panel // 2
+    g_chunk = 2 * (panel // n_col) // n_row
     scratch = [
         vmem((rows, width), BF16),
         vmem((n_panels, panel, panel), F32),
@@ -461,7 +478,7 @@
         vmem((2, n_rb, own, R_TILE), BF16),
         vmem((n_rb, own, R_TILE), BF16),
         vmem((n_rb, own, R_TILE), BF16),
-        vmem((2, n_row, half // n_row, panel), BF16),
+        vmem((n_col, n_row, g_chunk, half), BF16),
         vmem((8, LANES), F32), vmem((n_y - 1, 8, LANES), F32),
         vmem((8, LANES), F32), vmem((n_z - 1, 8, LANES), F32),
         vmem((2, n_row, chunk, panel), BF16),
@@ -469,18 +486,17 @@
         vmem((2, n_z, chunk, panel), BF16),
         vmem((2, n_z - 1, chunk, panel), BF16),
         vmem((2, n_row, chunk, panel), BF16),
-        vmem((n_row, half // n_row, panel), BF16),
-        vmem((n_y - 1, n_z, half // n_row, panel), BF16),
-        vmem((n_z, half // n_row, panel), BF16),
-        vmem((n_z - 1, half // n_row, panel), BF16),
-        vmem((n_row, half // n_row, panel), BF16),
-        dma((3,)), dma((3,)), dma((3,)),
-        dma((2, n_rb)), dma((2, n_rb)), dma((n_rb,)), dma((n_rb,)), dma, dma,
+        vmem((n_row, g_chunk, half), BF16),
+        vmem((n_y - 1, n_z, g_chunk, half), BF16),
+        vmem((n_z, g_chunk, half), BF16),
+        vmem((n_z - 1, g_chunk, half), BF16),
+        vmem((n_row, g_chunk, half), BF16),
+        dma((3,)), dma((5,)), dma((5,)),
+        dma((2, n_rb)), dma((2, n_rb)), dma((n_rb,)), dma((n_rb,)), dma((3,)), dma((3,)),
         dma((n_y - 1,)), dma((n_y - 1,)), dma((n_z - 1,)), dma((n_z - 1,)),
         dma((3, n_y - 1)), dma((3, n_y - 1)),
         dma((3, n_z - 1)), dma((3, n_z - 1)),
-        dma((3, n_z - 1)), dma((3, n_z - 1)),
-        dma((3, n_y - 1)), dma((3, n_y - 1)), pltpu.SemaphoreType.REGULAR((2,)),
+        dma((3, n_row - 1)), dma((3, n_row - 1)), pltpu.SemaphoreType.REGULAR((2,)),
     ]
     any_spec, vmem_spec = pl.BlockSpec(memory_space=pl.ANY), pl.BlockSpec(memory_space=pltpu.VMEM)
     return pl.pallas_call(

time: 68 us -> 65.4 us (0.962)
  the two profiles are of different devices: /device:TPU:4 before, /device:TPU:1 now
where the time goes in v4:
time: 65.4 us; the launch traced here: 65.2 us
  Pallas kernels  63.4 us (97%)
  local copies, waits for them, and re-layouts  1.87 us (3%)
    pallas_call x1, Pallas kernels, per_device(): pl.pallas_call(functools.partial(kernel, cfg), out_shape=jax.ShapeDtypeSt...  63.4 us
    unnamed x1, local copies, waits for them, and re-layouts  1.87 us

profile of v4, /device:TPU:1, one launch (start us, length us, event | category | flops | bytes accessed | tf_op | source)
XLA Modules:
  0.0 65.2 jit_solution(9942504553155808947)
XLA Ops:
  0.0 63.4 %shard_map.91 = bf16[1,256,1024]{2,1,0:T(8,128)(2,1)} custom-call(bf16[1,1024,4096]{2,1,0:T(8,128)(2,1)} %old_hbm.1, bf16[1,2,1024,128]{3,2,1,0:T(8,128)(2,1)} %refl_hbm.1, f32[1,2,512,512]{3,2,1,0:T(8,128)} %tri_hbm.1, f32[256,128]{1,0:T(8,128)} %bitcast.6, f32[256,128]{1,0:T(8,128)} %bitcast.7, s32[256,128]{1,0:T(8,128)} %bitcast.8, s32[256,128]{1,0:T(8,128)} %bitcast.9, ...), custom_call_target="tpu_custom_call" | custom-call | tf_op jit(solution)/shard_map/pallas_call | solution.py:502
  63.4 1.9 %copy.11 = bf16[1,256,1024]{2,1,0:T(8,128)(2,1)} copy(bf16[1,256,1024]{2,1,0:T(8,128)(2,1)} %shard_map.91) | data formatting | bytes 1048576

commit v5 on v4

--- a/solution.py
+++ b/solution.py
@@ -393,16 +393,6 @@
     for copy in sz_copies:
         copy.start()
 
-    red_proj[0][1]()
-    red_proj[1][1]()
-
-    def apply_triangle(value, p):
-        high = value.astype(BF16).astype(F32)
-        stacked = jnp.concatenate([high, value - high], axis=0).astype(BF16)
-        by_hi = dot(stacked, u_hi[p], NT)
-        by_lo = dot(stacked, u_lo[p], NT)
-        return (by_hi[:chunk] + (by_hi[chunk:] + by_lo[:chunk])).astype(BF16)
-
     red_gram[4]()
     diagonal = {"col": (1 - x) * 2 + 1 - core}
     gram_copies = [
@@ -412,6 +402,16 @@
     for copy in gram_copies:
         copy.start()
     gram_all[col] = g_all[...]
+    red_proj[0][1]()
+    red_proj[1][1]()
+
+    def apply_triangle(value, p):
+        high = value.astype(BF16).astype(F32)
+        stacked = jnp.concatenate([high, value - high], axis=0).astype(BF16)
+        by_hi = dot(stacked, u_hi[p], NT)
+        by_lo = dot(stacked, u_lo[p], NT)
+        return (by_hi[:chunk] + (by_hi[chunk:] + by_lo[:chunk])).astype(BF16)
+
     coef_1 = apply_triangle(red_proj[0][2](), 1)
     red_proj[0][3](coef_1)
     gram_rows = []

time: 65.4 us -> 64.1 us (0.980)
  the two profiles are of different devices: /device:TPU:1 before, /device:TPU:4 now
where the time goes in v5:
time: 64.1 us; the launch traced here: 64 us
  Pallas kernels  62.1 us (97%)
  local copies, waits for them, and re-layouts  1.87 us (3%)
    pallas_call x1, Pallas kernels, per_device(): pl.pallas_call(functools.partial(kernel, cfg), out_shape=jax.ShapeDtypeSt...  62.1 us
    unnamed x1, local copies, waits for them, and re-layouts  1.87 us

profile of v5, /device:TPU:4, one launch (start us, length us, event | category | flops | bytes accessed | tf_op | source)
XLA Modules:
  0.0 64.0 jit_solution(16816733831435385747)
XLA Ops:
  0.0 62.1 %shard_map.91 = bf16[1,256,1024]{2,1,0:T(8,128)(2,1)} custom-call(bf16[1,1024,4096]{2,1,0:T(8,128)(2,1)} %old_hbm.1, bf16[1,2,1024,128]{3,2,1,0:T(8,128)(2,1)} %refl_hbm.1, f32[1,2,512,512]{3,2,1,0:T(8,128)} %tri_hbm.1, f32[256,128]{1,0:T(8,128)} %bitcast.6, f32[256,128]{1,0:T(8,128)} %bitcast.7, s32[256,128]{1,0:T(8,128)} %bitcast.8, s32[256,128]{1,0:T(8,128)} %bitcast.9, ...), custom_call_target="tpu_custom_call" | custom-call | tf_op jit(solution)/shard_map/pallas_call | solution.py:502
  62.1 1.9 %copy.11 = bf16[1,256,1024]{2,1,0:T(8,128)(2,1)} copy(bf16[1,256,1024]{2,1,0:T(8,128)(2,1)} %shard_map.91) | data formatting | bytes 1048576

commit v6 on v5

--- a/solution.py
+++ b/solution.py
@@ -236,11 +236,11 @@
     def reduction(i, buf, from_y, z_in, from_z, everything):
         y_out = [
             remote(buf.at[pl.ds(y_peer(d) * n_z, n_z)], from_y.at[d - 1], ys_sem.at[i, d - 1], yr_sem.at[i, d - 1], y_dev(d))
-            for d in range(1, n_y)
+            for d in sorted(range(1, n_y), key=lambda d: -min(d, n_y - d))
         ]
         z_out = [
             remote(z_in.at[z_peer(d)], from_z.at[d - 1], zs_sem.at[i, d - 1], zr_sem.at[i, d - 1], z_dev(d))
-            for d in range(1, n_z)
+            for d in sorted(range(1, n_z), key=lambda d: -min(d, n_z - d))
         ]
         mine = everything.at[row]
         back = [remote(mine, mine, b_ssem.at[i, k], b_rsem.at[i, k], far_dev(dy, dz)) for k, (dy, dz) in enumerate(far)]

time: 64.1 us -> 64.2 us (level)
  no operation moved by 1% of the time
where the time goes in v6:
time: 64.2 us; the launch traced here: 64 us
  Pallas kernels  62.2 us (97%)
  local copies, waits for them, and re-layouts  1.87 us (3%)
    pallas_call x1, Pallas kernels, per_device(): pl.pallas_call(functools.partial(kernel, cfg), out_shape=jax.ShapeDtypeSt...  62.2 us
    unnamed x1, local copies, waits for them, and re-layouts  1.87 us

profile of v6, /device:TPU:4, one launch (start us, length us, event | category | flops | bytes accessed | tf_op | source)
XLA Modules:
  0.0 64.0 jit_solution(14511806288905207708)
XLA Ops:
  0.0 62.2 %shard_map.91 = bf16[1,256,1024]{2,1,0:T(8,128)(2,1)} custom-call(bf16[1,1024,4096]{2,1,0:T(8,128)(2,1)} %old_hbm.1, bf16[1,2,1024,128]{3,2,1,0:T(8,128)(2,1)} %refl_hbm.1, f32[1,2,512,512]{3,2,1,0:T(8,128)} %tri_hbm.1, f32[256,128]{1,0:T(8,128)} %bitcast.6, f32[256,128]{1,0:T(8,128)} %bitcast.7, s32[256,128]{1,0:T(8,128)} %bitcast.8, s32[256,128]{1,0:T(8,128)} %bitcast.9, ...), custom_call_target="tpu_custom_call" | custom-call | tf_op jit(solution)/shard_map/pallas_call | solution.py:502
  62.2 1.9 %copy.11 = bf16[1,256,1024]{2,1,0:T(8,128)(2,1)} copy(bf16[1,256,1024]{2,1,0:T(8,128)(2,1)} %shard_map.91) | data formatting | bytes 1048576
